TPU v7x, 512 devices: a whole 4x4x16 slice. The times are simulated.
512 devices in a mesh: row: 64 (over y, z), col: 8 (over x, core).
Axes of the slice: x: 4, y: 4, z: 16, core: 2. Of those that a mesh axis runs over, the one named last changes fastest.
Arguments:
- kernel: bfloat16 [328, 64, 8, 2624], P(None, 'row', 'col'), may hold values from -1 to 8, as said below
Outputs:
- factored: float32 [328, 64, 8, 2624], P(None, 'row', 'col')
Inputs may be any that keep to these rules, and one draw needn't show every extreme that they name: kernel is symmetric (entry i, j equals entry j, i), and its leading 2 * 256 rows and columns form a positive definite matrix.
All inputs are finite; a program needn't handle non-finite values.
Results may differ from a plain program's by a relative error of at most 0.0086.
Values may be sent and summed in bfloat16 or wider, within the bound.
No kernel may reach another device: no remote copies, remote signals or barrier semaphores. Data moves between devices by JAX's collectives and lax.ppermute only.
A program may use at most 64 MiB of HBM per device.

v0:
```python
import jax
import jax.numpy as jnp
from jax import lax
from jax.sharding import PartitionSpec as P

B = 256
STEPS = 2


def contract_last(left, right):
    return lax.dot_general(
        left, right, (((1,), (1,)), ((), ())), preferred_element_type=jnp.float32
    )


def on_device(kernel):
    row_count = lax.axis_size("row")
    col_count = lax.axis_size("col")
    row_index = lax.axis_index("row")
    col_index = lax.axis_index("col")
    rows_each = B // row_count
    cols_each = B // col_count
    work = kernel[:, 0, 0, :].astype(jnp.float32)
    eye = jnp.eye(B, dtype=jnp.float32)
    for step in range(STEPS):
        row_start = step * rows_each
        row_end = row_start + rows_each
        col_start = step * cols_each
        col_end = col_start + cols_each
        piece = work[row_start:row_end, col_start:col_end].reshape(rows_each, 1, cols_each)
        gathered = lax.all_gather(piece, ("row", "col"), axis=1, tiled=True)
        corner = jnp.transpose(
            gathered.reshape(rows_each, row_count, col_count, cols_each), (0, 1, 3, 2)
        ).reshape(B, B)
        factor = jnp.linalg.cholesky(corner)
        inverse_b = jax.scipy.linalg.solve_triangular(factor, eye, lower=True).astype(jnp.bfloat16)
        column_b = work[row_end:, col_start:col_end].astype(jnp.bfloat16)[:, :, None]
        column_all = lax.all_gather(column_b, "col", axis=2, tiled=True).reshape(-1, B)
        solved = contract_last(column_all, inverse_b)
        inverse_cube = inverse_b.reshape(B, rows_each, row_count)
        row_b = work[row_start:row_end, col_end:].astype(jnp.bfloat16)[:, None, :]
        group_rows = lax.all_gather(row_b, "row", axis=1, tiled=True)
        count = group_rows.shape[1]
        block = inverse_cube.reshape(B, rows_each * count)
        transposed = jnp.dot(
            block, group_rows.reshape(rows_each * count, -1), preferred_element_type=jnp.float32
        )
        solved_b = solved.astype(jnp.bfloat16)
        transposed_b = transposed.astype(jnp.bfloat16)
        trailing = work[row_end:, col_end:] - jnp.dot(
            solved_b, transposed_b, preferred_element_type=jnp.float32
        )
        work = work.at[row_end:, col_end:].set(trailing)
        own_rows = lax.dynamic_index_in_dim(
            factor.reshape(rows_each, row_count, cols_each, col_count), row_index, 1, keepdims=False
        )
        own_factor = lax.dynamic_index_in_dim(own_rows, col_index, 2, keepdims=False)
        own_solved = lax.dynamic_index_in_dim(
            solved.reshape(-1, cols_each, col_count), col_index, 2, keepdims=False
        )
        own_transposed = lax.dynamic_index_in_dim(
            transposed.reshape(rows_each, row_count, -1), row_index, 1, keepdims=False
        )
        work = work.at[row_start:row_end, col_start:col_end].set(own_factor)
        work = work.at[row_end:, col_start:col_end].set(own_solved)
        work = work.at[row_start:row_end, col_end:].set(own_transposed)
    return work[:, None, None, :]


def solution(mesh):
    in_specs = (P(None, "row", "col", None),)
    out_specs = P(None, "row", "col", None)
    return jax.shard_map(
        on_device, mesh=mesh, in_specs=in_specs, out_specs=out_specs, check_vma=False
    )
```

profile of v0, /device:TPU:4, one launch (start us, length us, event | category | flops | bytes accessed | tf_op | source)
XLA Modules:
  0.0 709.6 jit_solution(3176731116045989935)
XLA Ops:
  12.3 140.0 %all-gather.4 = f32[512,32,4]{1,2,0:T(4,128)S(1)} all-gather(f32[1,32,4]{1,2,0:T(4,128)S(1)} %slice_bitcast_fusion.12), channel_id=2, replica_groups=mesh['row'=64,'col'=8] {'row','col'}, dimensions={0}, use_global_device_ids=true | all-gather | bytes 262656 | tf_op jit(solution)/shard_map/all_gather | solution.py:31
  166.8 13.2 %cholesky.130 = f32[128,128]{1,0:T(8,128)} custom-call(f32[128,128]{1,0:T(8,128)} %cholesky.194), custom_call_target="Cholesky" | custom-call | tf_op jit(solution)/shard_map/jit(cholesky)/cholesky | solution.py:35
  181.4 11.3 %custom-call.13 = f32[1,128,128]{1,2,0:T(8,128)} custom-call(f32[1,128,128]{2,1,0:T(8,128)} %get-tuple-element.150), custom_call_target="InvertDiagBlocksLowerTriangular" | custom-call | tf_op jit(solution)/shard_map/jit(cholesky)/cholesky | solution.py:35
  197.7 13.5 %cholesky.147 = f32[128,128]{1,0:T(8,128)} custom-call(f32[128,128]{1,0:T(8,128)} %convolution_subtract_fusion.5), custom_call_target="Cholesky" | custom-call | tf_op jit(solution)/shard_map/jit(cholesky)/cholesky | solution.py:35
  218.9 7.0 while.12
  225.9 21.1 %custom-call.14 = f32[2,128,128]{1,2,0:T(8,128)} custom-call(f32[2,128,128]{2,1,0:T(8,128)} %get-tuple-element.117), custom_call_target="InvertDiagBlocksLowerTriangular" | custom-call | tf_op jit(solution)/shard_map/jit(_solve_triangular)/triangular_solve | solution.py:36
  251.4 11.6 %all_gather.19 = bf16[324,32,8]{0,1,2:T(8,128)(2,1)S(1)} all-gather(bf16[324,32,1]{0,1,2:T(8,128)(2,1)S(1)} %copy.33), channel_id=1, replica_groups=mesh['row'=64,'col'=8] {'col'}, dimensions={2}, use_global_device_ids=true | all-gather | bytes 186624 | tf_op jit(solution)/shard_map/all_gather | solution.py:38
  277.9 4.1 reshape.384
  290.5 3.8 reshape.331
  294.3 3.6 fusion.31
  301.3 4.7 convolution_subtract_fusion
  307.6 18.0 %scatter.26 = f32[328,2624]{1,0:T(8,128)S(1)} dynamic-update-slice(f32[328,2624]{1,0:T(8,128)S(1)} %bitcast_convert_fusion, f32[324,2592]{1,0:T(8,128)} %convolution_subtract_fusion, s32[]{:T(128)} %constant.335.clone.1, s32[]{:T(128)} %constant.336.clone.1) | dynamic-update-slice | bytes 6718468 | tf_op jit(solution)/shard_map/scatter | solution.py:53
  332.1 3.9 scatter.31
  337.5 130.4 %all-gather.6 = f32[512,32,4]{1,2,0:T(4,128)S(1)} all-gather(f32[1,32,4]{1,2,0:T(4,128)S(1)} %slice_bitcast_fusion.11), channel_id=4, replica_groups=mesh['row'=64,'col'=8] {'row','col'}, dimensions={0}, use_global_device_ids=true | all-gather | bytes 262656 | tf_op jit(solution)/shard_map/all_gather | solution.py:31
  482.4 13.2 %cholesky.164 = f32[128,128]{1,0:T(8,128)} custom-call(f32[128,128]{1,0:T(8,128)} %cholesky.197), custom_call_target="Cholesky" | custom-call | tf_op jit(solution)/shard_map/jit(cholesky)/cholesky | solution.py:35
  497.0 11.3 %custom-call.15 = f32[1,128,128]{1,2,0:T(8,128)} custom-call(f32[1,128,128]{2,1,0:T(8,128)} %get-tuple-element.146), custom_call_target="InvertDiagBlocksLowerTriangular" | custom-call | tf_op jit(solution)/shard_map/jit(cholesky)/cholesky | solution.py:35
  513.3 13.4 %cholesky.181 = f32[128,128]{1,0:T(8,128)} custom-call(f32[128,128]{1,0:T(8,128)} %convolution_subtract_fusion.4), custom_call_target="Cholesky" | custom-call | tf_op jit(solution)/shard_map/jit(cholesky)/cholesky | solution.py:35
  536.6 7.0 while.13
  543.5 21.1 %custom-call.16 = f32[2,128,128]{1,2,0:T(8,128)} custom-call(f32[2,128,128]{2,1,0:T(8,128)} %get-tuple-element.118), custom_call_target="InvertDiagBlocksLowerTriangular" | custom-call | tf_op jit(solution)/shard_map/jit(_solve_triangular)/triangular_solve | solution.py:36
  571.7 12.8 %all_gather.21 = bf16[320,32,8]{0,1,2:T(8,128)(2,1)S(1)} all-gather(bf16[320,32,1]{0,1,2:T(8,128)(2,1)S(1)} %copy.41), channel_id=1, replica_groups=mesh['row'=64,'col'=8] {'col'}, dimensions={2}, use_global_device_ids=true | all-gather | bytes 184320 | tf_op jit(solution)/shard_map/all_gather | solution.py:38
  594.9 69.3 %all-gather.10.cloned.1.call-done = bf16[4,163840]{1,0:T(4,128)(2,1)} async-done(((bf16[4,2560]{1,0:T(4,128)(2,1)}), bf16[4,163840]{1,0:T(4,128)(2,1)}) %all-gather.10.cloned.1.call-update) | async-done | bytes 1310736 | tf_op jit(solution)/shard_map/all_gather | solution.py:42
  664.2 3.5 reshape.344
  673.1 17.3 %scatter.34 = f32[328,1,1,2624]{3,0,2,1:T(8,128)S(1)} dynamic-update-slice(f32[328,1,1,2624]{3,0,2,1:T(8,128)S(1)} %bitcast.132, f32[320,1,1,2560]{3,0,2,1:T(8,128)} %fusion, s32[]{:T(128)} %constant.343.clone.1, s32[]{:T(128)} %constant.337.clone.1, s32[]{:T(128)} %constant.337.clone.1, s32[]{:T(128)} %constant.340.clone.1) | dynamic-update-slice | bytes 6553604 | tf_op jit(solution)/shard_map/scatter | solution.py:53
  697.0 5.4 copy.51
  (124 shorter events, 146.5 us)
Async XLA Ops:
  6.5 268.8 %all-gather.12.cloned.1.call-start = ((), (), s32[]{:S(2)}) async-start(), calls=%async_computation.1 | async-start | bytes 1397760 | tf_op jit(solution)/shard_map/all_gather | solution.py:42
  8.0 656.2 %all-gather.10.cloned.1.call-start = ((), (), s32[]{:S(2)}) async-start(), calls=%async_computation | async-start | bytes 1331200 | tf_op jit(solution)/shard_map/all_gather | solution.py:42
  165.5 0.7 copy-start.4
  225.9 23.1 %copy-start.8 = (s32[2,2]{1,0:T(2,128)}, s32[2,2]{1,0:T(2,128)S(1)}, u32[]{:S(2)}) copy-start(s32[2,2]{1,0:T(2,128)S(1)} %get-tuple-element.257) | copy-start | bytes 52
  263.0 1.2 copy-start.1
  264.3 2.3 copy-start.2
  266.6 0.6 copy-start.6
  476.1 60.4 %copy-start.9 = (s32[2,2]{1,0:T(2,128)S(1)}, s32[2,2]{1,0:T(2,128)}, u32[]{:S(2)}) copy-start(s32[2,2]{1,0:T(2,128)} %copy-done.8) | copy-start | bytes 52
  481.0 0.7 copy-start.5
  585.8 2.4 copy-start.3
  588.2 0.6 copy-start.7
  667.7 2.0 copy-start
Sparse Core Ops, SparseCore 0:
  10.3 144.5 all-gather.11
  528.3 135.8 all-gather.9
where the time goes:
time: 723 us; the launch traced here: 710 us
  blocking collectives  295 us (41%)
  local copies, waits for them, and re-layouts  160 us (22%)
  other arithmetic  139 us (19%)
  waiting for transfers between devices  69.4 us (10%)
  matrix products  29 us (4%)
  between operations  16.6 us (2%)
    all_gather x2, blocking collectives, on_device(): gathered = lax.all_gather(piece, ('row', 'col'), axis=1, tiled=True)  270 us
    another operation x13, other arithmetic, on_device(): factor = jnp.linalg.cholesky(corner)  83.7 us
    all_gather x2, waiting for transfers between devices, on_device(): group_rows = lax.all_gather(row_b, 'row', axis=1, tiled=True)  69.3 us
    another operation x5, other arithmetic, on_device(): jax.scipy.linalg.solve_triangular(factor, eye, lower=True)  45.7 us
    scatter x2, local copies, waits for them, and re-layouts, on_device(): work = work.at[row_end:, col_end:].set(trailing)  35.4 us
    all_gather x2, blocking collectives, on_device(): lax.all_gather(column_b, 'col', axis=2, tiled=True).reshape(-1, B)  24.4 us
    unnamed x30, local copies, waits for them, and re-layouts  22.2 us
    another operation x15, local copies, waits for them, and re-layouts, on_device(): jax.scipy.linalg.solve_triangular(factor, eye, lower=True)  15.3 us
  transfers between devices with their start and end apart: 2, of which 1 were waited for; matrix products, arithmetic and copies ran while one was open for 23% of the time, Pallas kernels for 0%

commit v1 on v0

v1 whole, which is shorter than its diff:
```python
import functools

import jax
import jax.numpy as jnp
import numpy as np
from jax import lax
from jax.experimental import pallas as pl
from jax.experimental.pallas import tpu as pltpu
from jax.sharding import Mesh, PartitionSpec as P

B = 256
STEPS = 2
T = STEPS * B
NB = 64
LANE = 128
NY, NZH, NZL, NX, NC = 4, 4, 4, 4, 2
ROWS, COLS = NY * NZH * NZL, NX * NC
LR, LC = T // ROWS, T // COLS
TILE = 384
HIGH = lax.Precision.HIGHEST
F32, BF16 = jnp.float32, jnp.bfloat16


def mm(a, b, ca=1, cb=0, precision=None):
    return lax.dot_general(
        a, b, (((ca,), (cb,)), ((), ())), precision=precision, preferred_element_type=F32
    )


def eliminate(block):
    row = lax.broadcasted_iota(jnp.int32, (NB, NB), 0)
    col = lax.broadcasted_iota(jnp.int32, (NB, NB), 1)
    eye = (row == col).astype(F32)
    full = jnp.concatenate([block, eye], axis=1)
    groups = NB // 8
    r = [full[8 * g : 8 * g + 8, :] for g in range(groups)]
    sub = lax.broadcasted_iota(jnp.int32, (8, 128), 0)
    scales = []
    for b in range(groups):
        c = [
            {g: jnp.broadcast_to(r[g][:, 8 * b + i : 8 * b + i + 1], (8, 128)) for g in range(b, groups)}
            for i in range(8)
        ]
        scale = jnp.zeros((8, 128), F32)
        for i in range(8):
            pivot = jnp.broadcast_to(c[i][b][i : i + 1, :], (8, 128))
            inv = 1.0 / pivot
            scale = jnp.where(sub == i, lax.rsqrt(pivot), scale)
            lead = jnp.broadcast_to(r[b][i : i + 1, :], (8, 128))
            ahead = {i2: jnp.broadcast_to(c[i2][b][i : i + 1, :], (8, 128)) for i2 in range(i + 1, 8)}
            for g in range(b, groups):
                m = c[i][g] * inv
                if g == b:
                    m = jnp.where(sub > i, m, 0.0)
                for i2 in range(i + 1, 8):
                    c[i2][g] = c[i2][g] - m * ahead[i2]
                r[g] = r[g] - m * lead
        scales.append(scale)
    out = jnp.concatenate([r[g] * scales[g] for g in range(groups)], axis=0)
    upper = jnp.where(row <= col, out[:, :NB], 0.0)
    lower = jnp.where(row >= col, out[:, NB:], 0.0)
    return upper, lower


def factor_panel(a):
    nb = B // NB
    cur = [[a[NB * i : NB * i + NB, NB * j : NB * j + NB] if i >= j else None for j in range(nb)] for i in range(nb)]
    up = [[None] * nb for _ in range(nb)]
    low = [[None] * nb for _ in range(nb)]
    inv = [[None] * nb for _ in range(nb)]
    zero = jnp.zeros((NB, NB), F32)
    for k in range(nb):
        u, g = eliminate(cur[k][k])
        up[k][k] = u
        inv[k][k] = g
        if k + 1 < nb:
            below = jnp.concatenate([cur[i][k] for i in range(k + 1, nb)], axis=0)
            solved = mm(below, g, 1, 1, HIGH)
            for i in range(k + 1, nb):
                low[i][k] = solved[NB * (i - k - 1) : NB * (i - k), :]
            upper = mm(g, below, 1, 1, HIGH)
            for i in range(k + 1, nb):
                up[k][i] = upper[:, NB * (i - k - 1) : NB * (i - k)]
            for j in range(k + 1, nb):
                prod = mm(solved[NB * (j - k - 1) :, :], low[j][k], 1, 1, HIGH)
                for i in range(j, nb):
                    cur[i][j] = cur[i][j] - prod[NB * (i - j) : NB * (i - j + 1), :]
        if k:
            left = jnp.concatenate(low[k][:k], axis=1)
            prev = jnp.concatenate(
                [jnp.concatenate([inv[i][j] if j <= i else zero for j in range(k)], axis=1) for i in range(k)], axis=0
            )
            row = -mm(g, mm(left, prev, 1, 0, HIGH), 1, 0, HIGH)
            for j in range(k):
                inv[k][j] = row[:, NB * j : NB * j + NB]
    upper = jnp.concatenate(
        [jnp.concatenate([up[i][j] if j >= i else zero for j in range(nb)], axis=1) for i in range(nb)], axis=0
    )
    inverse = jnp.concatenate(
        [jnp.concatenate([inv[i][j] if j <= i else zero for j in range(nb)], axis=1) for i in range(nb)], axis=0
    )
    return upper, inverse


def factor_kernel(pos_ref, x_ref, prow_ref, pcol_ref, head_ref, g_ref, l_ref, own_ref, u_scr, a_scr):
    acc = None
    for y in range(NY):
        flat = jnp.concatenate([x_ref[y, k] for k in range(COLS)], axis=1)
        part = mm(flat, pcol_ref[...]).astype(BF16)
        rows = NZH * NZL * LR
        term = mm(prow_ref[:, rows * y : rows * y + rows], part)
        acc = term if acc is None else acc + term
    a_scr[...] = acc
    u1, g1 = factor_panel(a_scr[0:B, 0:B])
    g1b = g1.astype(BF16)
    s21 = mm(a_scr[B:T, 0:B].astype(BF16), g1b, 1, 1)
    s12 = mm(g1b, a_scr[0:B, B:T].astype(BF16), 1, 0)
    s21b = s21.astype(BF16)
    a22 = a_scr[B:T, B:T] - mm(s21b, s21b, 1, 1)
    u2, g2 = factor_panel(a22)
    g2b = g2.astype(BF16)
    g_ref[0] = g1b
    g_ref[1] = g2b
    l_ref[...] = s21b
    head_ref[0:B, :] = mm(g1b, prow_ref[0:B, :]).astype(BF16)
    head_ref[B:T, :] = prow_ref[B:T, :]
    for k in range(B // LANE):
        lanes = slice(LANE * k, LANE * k + LANE)
        u_scr[k, 0:B, :] = u1.T[:, lanes]
        u_scr[k, B:T, :] = s21[:, lanes]
        u_scr[B // LANE + k, 0:B, :] = s12[:, lanes]
        u_scr[B // LANE + k, B:T, :] = u2.T[:, lanes]
    r = pos_ref[0]
    q = pos_ref[1]
    own = jnp.concatenate([u_scr[k, pl.ds(r, LR, stride=ROWS), :] for k in range(T // LANE)], axis=1)
    pick = (
        lax.broadcasted_iota(jnp.int32, (T, LC), 0) == lax.broadcasted_iota(jnp.int32, (T, LC), 1) * COLS + q
    ).astype(F32)
    own_ref[...] = mm(own, pick, 1, 0, HIGH)


def update_kernel(pos_ref, head_ref, g_ref, l_ref, own_ref, wr_ref, x_ref, w_ref, out_ref, srow, scol, u_scr):
    step = pl.program_id(0)
    l21 = l_ref[...]

    @pl.when(step == 0)
    def _():
        q = pos_ref[1]
        s1 = mm(wr_ref[:, 0:B], g_ref[0], 1, 1)
        s1b = s1.astype(BF16)
        c2 = (wr_ref[:, B:T].astype(F32) - mm(s1b, l21, 1, 1)).astype(BF16)
        s2 = mm(c2, g_ref[1], 1, 1)
        srow[:, 0:B] = s1b
        srow[:, B:T] = s2.astype(BF16)
        pick = (
            lax.broadcasted_iota(jnp.int32, (B, LC // 2), 0)
            == lax.broadcasted_iota(jnp.int32, (B, LC // 2), 1) * COLS + q
        ).astype(F32)
        scol[:, 0 : LC // 2] = mm(s1, pick, 1, 0, HIGH)
        scol[:, LC // 2 : LC] = mm(s2, pick, 1, 0, HIGH)

    both = mm(head_ref[...], x_ref[...])
    u1 = both[0:B, :]
    u1b = u1.astype(BF16)
    c2 = (both[B:T, :] - mm(l21, u1b)).astype(BF16)
    u2 = mm(g_ref[1], c2)
    for k in range(TILE // LANE):
        u_scr[k, 0:B, :] = u1[:, LANE * k : LANE * k + LANE]
        u_scr[k, B:T, :] = u2[:, LANE * k : LANE * k + LANE]
    ub = jnp.concatenate([u1b, u2.astype(BF16)], axis=0)
    out_ref[...] = w_ref[...].astype(F32) - mm(srow[...], ub)
    for k in range(TILE // LANE):
        out_ref[0:LR, LANE * k : LANE * k + LANE] = u_scr[k, pl.ds(pos_ref[0], LR, stride=ROWS), :]

    @pl.when(step == 0)
    def _():
        out_ref[:, 0:LC] = scol[...]
        out_ref[0:LR, 0:LC] = own_ref[...]


def permutations():
    nat = np.arange(T)
    prow = np.zeros((T, T), np.float32)
    stored = (nat % ROWS) * LR + nat // ROWS
    prow[nat, stored] = 1
    pcol = np.zeros((T, T), np.float32)
    pcol[(nat % COLS) * LC + nat // COLS, nat] = 1
    return prow.astype(jnp.bfloat16), pcol.astype(jnp.bfloat16)


def factor(pos, corner, prow, pcol):
    vmem = pl.BlockSpec(memory_space=pltpu.VMEM)
    return pl.pallas_call(
        factor_kernel,
        out_shape=(
            jax.ShapeDtypeStruct((T, T), BF16),
            jax.ShapeDtypeStruct((STEPS, B, B), BF16),
            jax.ShapeDtypeStruct((B, B), BF16),
            jax.ShapeDtypeStruct((LR, LC), F32),
        ),
        in_specs=[pl.BlockSpec(memory_space=pltpu.SMEM), vmem, vmem, vmem],
        out_specs=(vmem, vmem, vmem, vmem),
        scratch_shapes=[pltpu.VMEM((T // LANE, T, LANE), F32), pltpu.VMEM((T, T), F32)],
        name="factor",
    )(pos, corner, prow, pcol)


def update(pos, head, g, l21, own, wr, x, w):
    rows, cols = w.shape
    whole = lambda *shape: pl.BlockSpec(shape, lambda i: (0,) * len(shape))
    return pl.pallas_call(
        update_kernel,
        grid=(pl.cdiv(cols, TILE),),
        out_shape=jax.ShapeDtypeStruct((rows, cols), F32),
        in_specs=[
            pl.BlockSpec(memory_space=pltpu.SMEM),
            whole(T, T),
            whole(STEPS, B, B),
            whole(B, B),
            whole(LR, LC),
            whole(rows, T),
            pl.BlockSpec((T, TILE), lambda i: (0, i)),
            pl.BlockSpec((rows, TILE), lambda i: (0, i)),
        ],
        out_specs=pl.BlockSpec((rows, TILE), lambda i: (0, i)),
        scratch_shapes=[
            pltpu.VMEM((rows, T), BF16),
            pltpu.VMEM((rows, LC), F32),
            pltpu.VMEM((TILE // LANE, T, LANE), F32),
        ],
        name="update",
    )(pos, head, g, l21, own, wr, x, w)


def everyone(x, axis, count):
    return lax.all_to_all(jnp.broadcast_to(x[None], (count,) + x.shape), axis, 0, 0, tiled=True)


def on_device(kernel):
    work = kernel[:, 0, 0, :]
    rows, cols = work.shape
    r = lax.axis_index(("y", "zh", "zl"))
    q = lax.axis_index(("x", "c"))
    pos = jnp.stack([r, q]).astype(jnp.int32)
    prow, pcol = permutations()
    prow, pcol = jnp.asarray(prow), jnp.asarray(pcol)
    head_rows = work[0:LR, :]

    corner = everyone(head_rows[:, 0:LC], ("zh", "zl"), NZH * NZL)
    corner = everyone(corner.reshape(NZH * NZL * LR, LC), ("y", "x", "c"), NY * COLS)
    corner = corner.reshape(NY, COLS, NZH * NZL * LR, LC)

    wr = everyone(work[:, 0:LC], ("x", "c"), COLS)
    wr = mm(jnp.transpose(wr, (1, 0, 2)).reshape(rows, T), pcol).astype(BF16)

    x = lax.all_gather(head_rows, ("zh", "zl"), axis=0, tiled=False)
    x = lax.all_gather(x.reshape(NZH * NZL * LR, cols), "y", axis=0, tiled=False)
    x = x.reshape(T, cols)

    head, g, l21, own = factor(pos, corner, prow, pcol)
    out = update(pos, head, g, l21, own, wr, x, work)
    return out[:, None, None, :]


def solution(mesh):
    inner = Mesh(mesh.devices.reshape(NY, NZH, NZL, NX, NC), ("y", "zh", "zl", "x", "c"))
    spec = P(None, ("y", "zh", "zl"), ("x", "c"), None)
    return jax.shard_map(on_device, mesh=inner, in_specs=(spec,), out_specs=spec, check_vma=False)
```

time: 723 us -> 153 us (0.21)
  the two profiles are of different devices: /device:TPU:4 before, /device:TPU:1 now
where the time goes in v1:
time: 153 us
  blocking collectives  35.7 us (23%)
  Pallas kernels  34.7 us (23%)
  waiting for transfers between devices  28.1 us (18%)
  starting transfers between devices  25.9 us (17%)
  between operations  13.5 us (9%)
  local copies, waits for them, and re-layouts  13.2 us (9%)
    all_gather x1, blocking collectives, on_device(): x = lax.all_gather(head_rows, ('zh', 'zl'), axis=0, tiled=False)  35.7 us
    all_to_all x3, waiting for transfers between devices, everyone(): lax.all_to_all(jnp.broadcast_to(x[None], (count,) + x.shape), axis, 0, 0,...  28.1 us
    all_to_all x3, starting transfers between devices, everyone(): lax.all_to_all(jnp.broadcast_to(x[None], (count,) + x.shape), axis, 0, 0,...  25.9 us
    pallas_call x1, Pallas kernels, factor(): pl.pallas_call(factor_kernel, out_shape=(jax.ShapeDtypeStruct((T, T), BF1...  23.4 us
    pallas_call x1, Pallas kernels, update(): pl.pallas_call(update_kernel, grid=(pl.cdiv(cols, TILE),), out_shape=jax....  11.4 us
    broadcast_in_dim x1, local copies, waits for them, and re-layouts, on_device(): return out[:, None, None, :]  7.41 us
  transfers between devices with their start and end apart: 4, of which 3 were waited for; matrix products, arithmetic and copies ran while one was open for 4% of the time, Pallas kernels for 15%

profile of v1, /device:TPU:1, one launch (start us, length us, event | category | flops | bytes accessed | tf_op | source)
XLA Modules:
  0.0 152.7 jit_solution(11348913385381470837)
XLA Ops:
  6.5 0.0 all-gather.4.cloned.1.call-start
  6.5 0.8 fusion.1
  7.4 35.7 %all-gather = bf16[128,1,1,2624]{3,0,2,1:T(8,128)(2,1)} all-gather(bf16[8,1,1,2624]{3,0,2,1:T(8,128)(2,1)S(1)} %get-tuple-element.13), channel_id=2, replica_groups=mesh['y'=4,'zh'=4,'zl'=4,'x'=4,'c'=2] {'zh','zl'}, dimensions={0}, use_global_device_ids=true | all-gather | bytes 713728 | tf_op jit(solution)/shard_map/all_gather | solution.py:256
  43.0 0.0 all-gather.4.cloned.1.call-update
  43.1 0.7 reshape.21
  43.8 6.2 %all-to-all-start = ((bf16[16,2,256]{2,1,0:T(2,128)(2,1)}), bf16[16,2,256]{2,1,0:T(2,128)(2,1)S(1)}, u32[]{:S(2)}, u32[]{:S(2)}) async-start(bf16[16,2,256]{2,1,0:T(2,128)(2,1)} %reshape.21), calls=%async_computation | async-start | bytes 32768 | tf_op jit(solution)/shard_map/all_to_all | solution.py:236
  50.0 0.9 slice.17
  50.9 0.1 copy.13
  51.0 10.4 %all-to-all-done = bf16[16,2,256]{2,1,0:T(2,128)(2,1)S(1)} async-done(((bf16[16,2,256]{2,1,0:T(2,128)(2,1)}), bf16[16,2,256]{2,1,0:T(2,128)(2,1)S(1)}, u32[]{:S(2)}, u32[]{:S(2)}) %all-to-all-start) | async-done | bytes 16416 | tf_op jit(solution)/shard_map/all_to_all | solution.py:236
  61.4 0.8 broadcast_in_dim.25
  62.2 13.6 %all-to-all-start.2 = ((bf16[8,328,64]{1,2,0:T(8,128)(2,1)}), bf16[8,328,64]{1,2,0:T(8,128)(2,1)S(1)}, u32[]{:S(2)}, u32[]{:S(2)}) async-start(bf16[8,328,64]{1,2,0:T(8,128)(2,1)} %broadcast_in_dim.25), calls=%async_computation.2 | async-start | bytes 786432 | tf_op jit(solution)/shard_map/all_to_all | solution.py:236
  75.8 0.1 reshape.22
  75.8 0.1 copy.11
  75.9 7.9 %all-to-all-done.2 = bf16[8,328,64]{1,2,0:T(8,128)(2,1)S(1)} async-done(((bf16[8,328,64]{1,2,0:T(8,128)(2,1)}), bf16[8,328,64]{1,2,0:T(8,128)(2,1)S(1)}, u32[]{:S(2)}, u32[]{:S(2)}) %all-to-all-start.2) | async-done | bytes 335904 | tf_op jit(solution)/shard_map/all_to_all | solution.py:236
  83.8 0.9 broadcast_in_dim.24
  84.7 6.1 %all-to-all-start.1 = ((bf16[32,128,64]{1,2,0:T(8,128)(2,1)}), bf16[32,128,64]{1,2,0:T(8,128)(2,1)S(1)}, u32[]{:S(2)}, u32[]{:S(2)}) async-start(bf16[32,128,64]{1,2,0:T(8,128)(2,1)} %broadcast_in_dim.24), calls=%async_computation.1 | async-start | bytes 1048576 | tf_op jit(solution)/shard_map/all_to_all | solution.py:236
  90.9 0.6 pad_add_fusion.pos_ref
  91.5 0.0 copy-done
  91.5 1.1 fusion.wr_ref
  92.6 9.8 %all-to-all-done.1 = bf16[32,128,64]{1,2,0:T(8,128)(2,1)S(1)} async-done(((bf16[32,128,64]{1,2,0:T(8,128)(2,1)}), bf16[32,128,64]{1,2,0:T(8,128)(2,1)S(1)}, u32[]{:S(2)}, u32[]{:S(2)}) %all-to-all-start.1) | async-done | bytes 524320 | tf_op jit(solution)/shard_map/all_to_all | solution.py:236
  102.4 1.3 copy.12
  103.7 23.4 %factor.1 = (bf16[512,512]{1,0:T(8,128)(2,1)}, bf16[2,256,256]{2,1,0:T(8,128)(2,1)}, bf16[256,256]{1,0:T(8,128)(2,1)}, f32[8,64]{1,0:T(8,128)}) custom-call(s32[2]{0:T(128)} %pad_add_fusion.pos_ref, bf16[4,8,128,64]{3,2,1,0:T(8,128)(2,1)} %bitcast.17, bf16[512,512]{1,0:T(8,128)(2,1)} %constant.27.clone.prow_ref.pcol_ref, ...), custom_call_target="tpu_custom_call" | custom-call | tf_op jit(solution)/shard_map/factor/pallas_call | solution.py:193
  127.1 11.4 %update.1 = f32[328,2624]{1,0:T(8,128)} custom-call(s32[2]{0:T(128)} %pad_add_fusion.pos_ref, bf16[512,512]{1,0:T(8,128)(2,1)} %get-tuple-element.9.head_ref, bf16[2,256,256]{2,1,0:T(8,128)(2,1)} %get-tuple-element.10.g_ref, bf16[256,256]{1,0:T(8,128)(2,1)} %get-tuple-element.11.l_ref, f32[8,64]{1,0:T(8,128)} %get-tuple-element.12.own_ref, ...), custom_call_target="tpu_custom_call" | custom-call | tf_op jit(solution)/shard_map/update/pallas_call | solution.py:211
  138.5 7.4 %copy.14 = f32[328,1,1,2624]{3,2,1,0:T(1,128)} copy(f32[328,1,1,2624]{3,0,2,1:T(8,128)} %bitcast.16) | data formatting | bytes 6885376 | tf_op jit(solution)/shard_map/broadcast_in_dim | solution.py:262
  (4 shorter events, 0.0 us)
Async XLA Ops:
  6.5 84.9 %copy-start = (bf16[512,512]{1,0:T(8,128)(2,1)S(1)}, bf16[512,512]{1,0:T(8,128)(2,1)}, u32[]{:S(2)}) copy-start(bf16[512,512]{1,0:T(8,128)(2,1)} %constant.27.clone.prow_ref.pcol_ref) | copy-start | bytes 1572868
  6.5 120.6 %all-gather.4.cloned.1.call-start = ((), (), s32[]{:S(2)}) async-start(), calls=%async_computation.3 | async-start | bytes 3440640 | tf_op jit(solution)/shard_map/all_gather | solution.py:257
  43.8 17.6 %all-to-all-start = ((bf16[16,2,256]{2,1,0:T(2,128)(2,1)}), bf16[16,2,256]{2,1,0:T(2,128)(2,1)S(1)}, u32[]{:S(2)}, u32[]{:S(2)}) async-start(bf16[16,2,256]{2,1,0:T(2,128)(2,1)} %reshape.21), calls=%async_computation | async-start | bytes 32768 | tf_op jit(solution)/shard_map/all_to_all | solution.py:236
  62.2 21.7 %all-to-all-start.2 = ((bf16[8,328,64]{1,2,0:T(8,128)(2,1)}), bf16[8,328,64]{1,2,0:T(8,128)(2,1)S(1)}, u32[]{:S(2)}, u32[]{:S(2)}) async-start(bf16[8,328,64]{1,2,0:T(8,128)(2,1)} %broadcast_in_dim.25), calls=%async_computation.2 | async-start | bytes 786432 | tf_op jit(solution)/shard_map/all_to_all | solution.py:236
  84.7 17.7 %all-to-all-start.1 = ((bf16[32,128,64]{1,2,0:T(8,128)(2,1)}), bf16[32,128,64]{1,2,0:T(8,128)(2,1)S(1)}, u32[]{:S(2)}, u32[]{:S(2)}) async-start(bf16[32,128,64]{1,2,0:T(8,128)(2,1)} %broadcast_in_dim.24), calls=%async_computation.1 | async-start | bytes 1048576 | tf_op jit(solution)/shard_map/all_to_all | solution.py:236
Sparse Core Ops, SparseCore 0:
  43.2 46.9 all-gather.3

commit v2 on v1

--- a/solution.py
+++ b/solution.py
@@ -13,7 +13,9 @@
 T = STEPS * B
 NB = 64
 LANE = 128
+FAR, NEAR = (4, -4, 8), (1, -1, 2)
 NY, NZH, NZL, NX, NC = 4, 4, 4, 4, 2
+NZ = NZH * NZL
 ROWS, COLS = NY * NZH * NZL, NX * NC
 LR, LC = T // ROWS, T // COLS
 TILE = 384
@@ -102,15 +104,32 @@
     return upper, inverse
 
 
-def factor_kernel(pos_ref, x_ref, prow_ref, pcol_ref, head_ref, g_ref, l_ref, own_ref, u_scr, a_scr):
-    acc = None
-    for y in range(NY):
-        flat = jnp.concatenate([x_ref[y, k] for k in range(COLS)], axis=1)
-        part = mm(flat, pcol_ref[...]).astype(BF16)
-        rows = NZH * NZL * LR
-        term = mm(prow_ref[:, rows * y : rows * y + rows], part)
-        acc = term if acc is None else acc + term
-    a_scr[...] = acc
+def natural_rows(r, absolute):
+    stored = lax.broadcasted_iota(jnp.int32, (B, T), 1)
+
+    def shift(place, table):
+        code = lax.rem(stored // place, 4)
+        out = jnp.zeros_like(code)
+        for k, d in enumerate(table):
+            out = jnp.where(code == k + 1, d, out)
+        return out
+
+    z = lax.rem(lax.rem(r, NZ) - shift(LR, FAR) - shift(4 * LR, NEAR) + 2 * NZ, NZ)
+    y = stored // (NZ * LR)
+    if not absolute:
+        y = lax.rem(r // NZ - shift(NZ * LR, NEAR) + 2 * NY, NY)
+    return lax.rem(stored, LR) * ROWS + y * NZ + z
+
+
+def factor_kernel(pos_ref, x_ref, pcol_ref, head_ref, g_ref, l_ref, own_ref, u_scr, a_scr):
+    r = pos_ref[0]
+    q = pos_ref[1]
+    rows = lax.broadcasted_iota(jnp.int32, (B, T), 0)
+    order = natural_rows(r, True)
+    prow = jnp.concatenate([(rows == order).astype(BF16), (rows + B == order).astype(BF16)], axis=0)
+    flat = jnp.concatenate([x_ref[y] for y in range(NY)], axis=1)
+    part = mm(pcol_ref[...], flat).astype(BF16)
+    a_scr[...] = mm(part, prow, 1, 1)
     u1, g1 = factor_panel(a_scr[0:B, 0:B])
     g1b = g1.astype(BF16)
     s21 = mm(a_scr[B:T, 0:B].astype(BF16), g1b, 1, 1)
@@ -122,16 +141,15 @@
     g_ref[0] = g1b
     g_ref[1] = g2b
     l_ref[...] = s21b
-    head_ref[0:B, :] = mm(g1b, prow_ref[0:B, :]).astype(BF16)
-    head_ref[B:T, :] = prow_ref[B:T, :]
+    order = natural_rows(r, False)
+    head_ref[0:B, :] = mm(g1b, (rows == order).astype(BF16)).astype(BF16)
+    head_ref[B:T, :] = (rows + B == order).astype(BF16)
     for k in range(B // LANE):
         lanes = slice(LANE * k, LANE * k + LANE)
         u_scr[k, 0:B, :] = u1.T[:, lanes]
         u_scr[k, B:T, :] = s21[:, lanes]
         u_scr[B // LANE + k, 0:B, :] = s12[:, lanes]
         u_scr[B // LANE + k, B:T, :] = u2.T[:, lanes]
-    r = pos_ref[0]
-    q = pos_ref[1]
     own = jnp.concatenate([u_scr[k, pl.ds(r, LR, stride=ROWS), :] for k in range(T // LANE)], axis=1)
     pick = (
         lax.broadcasted_iota(jnp.int32, (T, LC), 0) == lax.broadcasted_iota(jnp.int32, (T, LC), 1) * COLS + q
@@ -139,7 +157,7 @@
     own_ref[...] = mm(own, pick, 1, 0, HIGH)
 
 
-def update_kernel(pos_ref, head_ref, g_ref, l_ref, own_ref, wr_ref, x_ref, w_ref, out_ref, srow, scol, u_scr):
+def update_kernel(pos_ref, head_ref, g_ref, l_ref, own_ref, wr_ref, x0_ref, x1_ref, x2_ref, x3_ref, w_ref, out_ref, srow, scol, u_scr):
     step = pl.program_id(0)
     l21 = l_ref[...]
 
@@ -159,7 +177,8 @@
         scol[:, 0 : LC // 2] = mm(s1, pick, 1, 0, HIGH)
         scol[:, LC // 2 : LC] = mm(s2, pick, 1, 0, HIGH)
 
-    both = mm(head_ref[...], x_ref[...])
+    x = jnp.concatenate([ref[...] for ref in (x0_ref, x1_ref, x2_ref, x3_ref)], axis=0)
+    both = mm(head_ref[...], x)
     u1 = both[0:B, :]
     u1b = u1.astype(BF16)
     c2 = (both[B:T, :] - mm(l21, u1b)).astype(BF16)
@@ -168,27 +187,24 @@
         u_scr[k, 0:B, :] = u1[:, LANE * k : LANE * k + LANE]
         u_scr[k, B:T, :] = u2[:, LANE * k : LANE * k + LANE]
     ub = jnp.concatenate([u1b, u2.astype(BF16)], axis=0)
-    out_ref[...] = w_ref[...].astype(F32) - mm(srow[...], ub)
+    out_ref[:, 0, 0, :] = w_ref[...].astype(F32) - mm(srow[...], ub)
     for k in range(TILE // LANE):
-        out_ref[0:LR, LANE * k : LANE * k + LANE] = u_scr[k, pl.ds(pos_ref[0], LR, stride=ROWS), :]
+        out_ref[0:LR, 0, 0, LANE * k : LANE * k + LANE] = u_scr[k, pl.ds(pos_ref[0], LR, stride=ROWS), :]
 
     @pl.when(step == 0)
     def _():
-        out_ref[:, 0:LC] = scol[...]
-        out_ref[0:LR, 0:LC] = own_ref[...]
-
-
-def permutations():
+        out_ref[:, 0, 0, 0:LC] = scol[...]
+        out_ref[0:LR, 0, 0, 0:LC] = own_ref[...]
+
+
+def column_order():
     nat = np.arange(T)
-    prow = np.zeros((T, T), np.float32)
-    stored = (nat % ROWS) * LR + nat // ROWS
-    prow[nat, stored] = 1
     pcol = np.zeros((T, T), np.float32)
-    pcol[(nat % COLS) * LC + nat // COLS, nat] = 1
-    return prow.astype(jnp.bfloat16), pcol.astype(jnp.bfloat16)
-
-
-def factor(pos, corner, prow, pcol):
+    pcol[nat, (nat % COLS) * LC + nat // COLS] = 1
+    return pcol.astype(jnp.bfloat16)
+
+
+def factor(pos, corner, pcol):
     vmem = pl.BlockSpec(memory_space=pltpu.VMEM)
     return pl.pallas_call(
         factor_kernel,
@@ -198,20 +214,20 @@
             jax.ShapeDtypeStruct((B, B), BF16),
             jax.ShapeDtypeStruct((LR, LC), F32),
         ),
-        in_specs=[pl.BlockSpec(memory_space=pltpu.SMEM), vmem, vmem, vmem],
+        in_specs=[pl.BlockSpec(memory_space=pltpu.SMEM), vmem, vmem],
         out_specs=(vmem, vmem, vmem, vmem),
         scratch_shapes=[pltpu.VMEM((T // LANE, T, LANE), F32), pltpu.VMEM((T, T), F32)],
         name="factor",
-    )(pos, corner, prow, pcol)
-
-
-def update(pos, head, g, l21, own, wr, x, w):
+    )(pos, corner, pcol)
+
+
+def update(pos, head, g, l21, own, wr, xs, w):
     rows, cols = w.shape
     whole = lambda *shape: pl.BlockSpec(shape, lambda i: (0,) * len(shape))
     return pl.pallas_call(
         update_kernel,
         grid=(pl.cdiv(cols, TILE),),
-        out_shape=jax.ShapeDtypeStruct((rows, cols), F32),
+        out_shape=jax.ShapeDtypeStruct((rows, 1, 1, cols), F32),
         in_specs=[
             pl.BlockSpec(memory_space=pltpu.SMEM),
             whole(T, T),
@@ -219,21 +235,26 @@
             whole(B, B),
             whole(LR, LC),
             whole(rows, T),
-            pl.BlockSpec((T, TILE), lambda i: (0, i)),
+            *[pl.BlockSpec((T // NY, TILE), lambda i: (0, i))] * NY,
             pl.BlockSpec((rows, TILE), lambda i: (0, i)),
         ],
-        out_specs=pl.BlockSpec((rows, TILE), lambda i: (0, i)),
+        out_specs=pl.BlockSpec((rows, 1, 1, TILE), lambda i: (0, 0, 0, i)),
         scratch_shapes=[
             pltpu.VMEM((rows, T), BF16),
             pltpu.VMEM((rows, LC), F32),
             pltpu.VMEM((TILE // LANE, T, LANE), F32),
         ],
         name="update",
-    )(pos, head, g, l21, own, wr, x, w)
+    )(pos, head, g, l21, own, wr, *xs, w)
 
 
 def everyone(x, axis, count):
     return lax.all_to_all(jnp.broadcast_to(x[None], (count,) + x.shape), axis, 0, 0, tiled=True)
+
+
+def spread(x, axis, count, shifts):
+    parts = [lax.ppermute(x, axis, [(i, (i + d) % count) for i in range(count)]) for d in shifts]
+    return [x] + parts
 
 
 def on_device(kernel):
@@ -242,24 +263,21 @@
     r = lax.axis_index(("y", "zh", "zl"))
     q = lax.axis_index(("x", "c"))
     pos = jnp.stack([r, q]).astype(jnp.int32)
-    prow, pcol = permutations()
-    prow, pcol = jnp.asarray(prow), jnp.asarray(pcol)
-    head_rows = work[0:LR, :]
-
-    corner = everyone(head_rows[:, 0:LC], ("zh", "zl"), NZH * NZL)
-    corner = everyone(corner.reshape(NZH * NZL * LR, LC), ("y", "x", "c"), NY * COLS)
-    corner = corner.reshape(NY, COLS, NZH * NZL * LR, LC)
-
-    wr = everyone(work[:, 0:LC], ("x", "c"), COLS)
-    wr = mm(jnp.transpose(wr, (1, 0, 2)).reshape(rows, T), pcol).astype(BF16)
-
-    x = lax.all_gather(head_rows, ("zh", "zl"), axis=0, tiled=False)
-    x = lax.all_gather(x.reshape(NZH * NZL * LR, cols), "y", axis=0, tiled=False)
-    x = x.reshape(T, cols)
-
-    head, g, l21, own = factor(pos, corner, prow, pcol)
-    out = update(pos, head, g, l21, own, wr, x, work)
-    return out[:, None, None, :]
+    pcol = jnp.asarray(column_order())
+    head_rows = jnp.pad(work[0:LR, :], ((0, 0), (0, -cols % LANE)))
+
+    x = jnp.concatenate(spread(head_rows, ("zh", "zl"), NZ, FAR), axis=0)
+    x = jnp.concatenate(spread(x, ("zh", "zl"), NZ, NEAR), axis=0)
+    corner = everyone(jnp.transpose(x[:, 0:LC]), ("y", "x", "c"), NY * COLS)
+    corner = corner.reshape(NY, T, NZ * LR)
+    xs = spread(x, "y", NY, NEAR)
+
+    mine, corner = lax.optimization_barrier((work[:, 0:LC], corner))
+    wr = everyone(jnp.transpose(mine), ("x", "c"), COLS).reshape(T, rows)
+    wr = mm(wr, pcol, 0, 1).astype(BF16)
+
+    head, g, l21, own = factor(pos, corner, pcol)
+    return update(pos, head, g, l21, own, wr, xs, work)
 
 
 def solution(mesh):

time: 153 us -> 120 us (0.78)
  the two profiles are of different devices: /device:TPU:1 before, /device:TPU:19 now
where the time goes in v2:
time: 120 us; the launch traced here: 119 us
  starting transfers between devices  70.7 us (59%)
  Pallas kernels  34.2 us (29%)
  waiting for transfers between devices  7.44 us (6%)
  local copies, waits for them, and re-layouts  4.81 us (4%)
    ppermute x9, starting transfers between devices, spread(): lax.ppermute(x, axis, [(i, (i + d) % count) for i in range(count)])  42.7 us
    all_to_all x2, starting transfers between devices, everyone(): lax.all_to_all(jnp.broadcast_to(x[None], (count,) + x.shape), axis, 0, 0,...  28 us
    pallas_call x1, Pallas kernels, factor(): pl.pallas_call(factor_kernel, out_shape=(jax.ShapeDtypeStruct((T, T), BF1...  22.4 us
    pallas_call x1, Pallas kernels, update(): pl.pallas_call(update_kernel, grid=(pl.cdiv(cols, TILE),), out_shape=jax....  11.9 us
    ppermute x9, waiting for transfers between devices, spread(): lax.ppermute(x, axis, [(i, (i + d) % count) for i in range(count)])  6.98 us
  transfers between devices with their start and end apart: 11, of which 3 were waited for; matrix products, arithmetic and copies ran while one was open for 3% of the time, Pallas kernels for 19%

profile of v2, /device:TPU:19, one launch (start us, length us, event | category | flops | bytes accessed | tf_op | source)
XLA Modules:
  0.0 119.1 jit_solution(15879290456422578038)
XLA Ops:
  0.0 0.8 slice_bitcast_fusion
  0.8 15.4 %collective-permute-start.2 = (bf16[8,2688]{1,0:T(8,128)(2,1)S(1)}, bf16[8,2688]{1,0:T(8,128)(2,1)S(1)}, u32[]{:S(2)}, u32[]{:S(2)}) collective-permute-start(bf16[8,2688]{1,0:T(8,128)(2,1)S(1)} %get-tuple-element.17), channel_id=1, source_target_pairs={{0,64},{8,72},{16,80},{24,88},{32,96},{40,104},{48,112},{56,120},{... | collective-permute-start | bytes 129032 | tf_op jit(solution)/shard_map/ppermute | solution.py:256
  16.2 1.9 %collective-permute-start.1 = (bf16[8,2688]{1,0:T(8,128)(2,1)S(1)}, bf16[8,2688]{1,0:T(8,128)(2,1)S(1)}, u32[]{:S(2)}, u32[]{:S(2)}) collective-permute-start(bf16[8,2688]{1,0:T(8,128)(2,1)S(1)} %get-tuple-element.17), channel_id=1, source_target_pairs={{0,96},{8,104},{16,112},{24,120},{32,0},{40,8},{48,16},{56,24},{64... | collective-permute-start | bytes 129032 | tf_op jit(solution)/shard_map/ppermute | solution.py:256
  18.2 7.3 %collective-permute-start = (bf16[8,2688]{1,0:T(8,128)(2,1)S(1)}, bf16[8,2688]{1,0:T(8,128)(2,1)S(1)}, u32[]{:S(2)}, u32[]{:S(2)}) collective-permute-start(bf16[8,2688]{1,0:T(8,128)(2,1)S(1)} %get-tuple-element.17), channel_id=1, source_target_pairs={{0,32},{8,40},{16,48},{24,56},{32,64},{40,72},{48,80},{56,88},{64,... | collective-permute-start | bytes 129032 | tf_op jit(solution)/shard_map/ppermute | solution.py:256
  25.5 1.7 %collective-permute-done = bf16[8,2688]{1,0:T(8,128)(2,1)S(1)} collective-permute-done((bf16[8,2688]{1,0:T(8,128)(2,1)S(1)}, bf16[8,2688]{1,0:T(8,128)(2,1)S(1)}, u32[]{:S(2)}, u32[]{:S(2)}) %collective-permute-start) | collective-permute-done | bytes 43040 | tf_op jit(solution)/shard_map/ppermute | solution.py:256
  27.2 4.9 %collective-permute-start.5 = (bf16[32,2688]{1,0:T(8,128)(2,1)S(1)}, bf16[32,2688]{1,0:T(8,128)(2,1)S(1)}, u32[]{:S(2)}, u32[]{:S(2)}) collective-permute-start(bf16[32,2688]{1,0:T(8,128)(2,1)S(1)} %pad_maximum_fusion), channel_id=1, source_target_pairs={{0,16},{8,24},{16,32},{24,40},{32,48},{40,56},{48,64},{56,72},{64,... | collective-permute-start | bytes 516104 | tf_op jit(solution)/shard_map/ppermute | solution.py:256
  32.1 2.0 %collective-permute-start.4 = (bf16[32,2688]{1,0:T(8,128)(2,1)S(1)}, bf16[32,2688]{1,0:T(8,128)(2,1)S(1)}, u32[]{:S(2)}, u32[]{:S(2)}) collective-permute-start(bf16[32,2688]{1,0:T(8,128)(2,1)S(1)} %pad_maximum_fusion), channel_id=1, source_target_pairs={{0,120},{8,0},{16,8},{24,16},{32,24},{40,32},{48,40},{56,48},{64,5... | collective-permute-start | bytes 516104 | tf_op jit(solution)/shard_map/ppermute | solution.py:256
  34.1 3.2 %collective-permute-start.3 = (bf16[32,2688]{1,0:T(8,128)(2,1)S(1)}, bf16[32,2688]{1,0:T(8,128)(2,1)S(1)}, u32[]{:S(2)}, u32[]{:S(2)}) collective-permute-start(bf16[32,2688]{1,0:T(8,128)(2,1)S(1)} %pad_maximum_fusion), channel_id=1, source_target_pairs={{0,8},{8,16},{16,24},{24,32},{32,40},{40,48},{48,56},{56,64},{64,7... | collective-permute-start | bytes 516104 | tf_op jit(solution)/shard_map/ppermute | solution.py:256
  37.4 5.3 %collective-permute-done.3 = bf16[32,2688]{1,0:T(8,128)(2,1)S(1)} collective-permute-done((bf16[32,2688]{1,0:T(8,128)(2,1)S(1)}, bf16[32,2688]{1,0:T(8,128)(2,1)S(1)}, u32[]{:S(2)}, u32[]{:S(2)}) %collective-permute-start.3) | collective-permute-done | bytes 172064 | tf_op jit(solution)/shard_map/ppermute | solution.py:256
  42.9 0.9 broadcast_in_dim.4
  43.9 10.4 %all-to-all-start = ((bf16[32,64,128]{2,1,0:T(8,128)(2,1)}), bf16[32,64,128]{2,1,0:T(8,128)(2,1)S(1)}, u32[]{:S(2)}, u32[]{:S(2)}) async-start(bf16[32,64,128]{2,1,0:T(8,128)(2,1)} %broadcast_in_dim.4), calls=%async_computation | async-start | bytes 1048576 | tf_op jit(solution)/shard_map/all_to_all | solution.py:252
  54.3 2.2 %collective-permute-start.8 = (bf16[128,2688]{1,0:T(8,128)(2,1)S(1)}, bf16[128,2688]{1,0:T(8,128)(2,1)S(1)}, u32[]{:S(2)}, u32[]{:S(2)}) collective-permute-start(bf16[128,2688]{1,0:T(8,128)(2,1)S(1)} %constant_dynamic-update-slice_fusion.x0_ref), channel_id=1, source_target_pairs={{0,256},{128,384},{256,0},{384,128},{1,257},{129,385},{257,1},{385... | collective-permute-start | bytes 2064392 | tf_op jit(solution)/shard_map/ppermute | solution.py:256
  56.5 3.8 %collective-permute-start.7 = (bf16[128,2688]{1,0:T(8,128)(2,1)S(1)}, bf16[128,2688]{1,0:T(8,128)(2,1)S(1)}, u32[]{:S(2)}, u32[]{:S(2)}) collective-permute-start(bf16[128,2688]{1,0:T(8,128)(2,1)S(1)} %constant_dynamic-update-slice_fusion.x0_ref), channel_id=1, source_target_pairs={{0,384},{128,0},{256,128},{384,256},{1,385},{129,1},{257,129},{385... | collective-permute-start | bytes 2064392 | tf_op jit(solution)/shard_map/ppermute | solution.py:256
  60.3 1.9 %collective-permute-start.6 = (bf16[128,2688]{1,0:T(8,128)(2,1)S(1)}, bf16[128,2688]{1,0:T(8,128)(2,1)}, u32[]{:S(2)}, u32[]{:S(2)}) collective-permute-start(bf16[128,2688]{1,0:T(8,128)(2,1)S(1)} %constant_dynamic-update-slice_fusion.x0_ref), channel_id=1, source_target_pairs={{0,128},{128,256},{256,384},{384,0},{1,129},{129,257},{257,385},{3... | collective-permute-start | bytes 2064392 | tf_op jit(solution)/shard_map/ppermute | solution.py:256
  62.2 0.9 slice.16
  63.1 0.5 all-to-all-done
  63.6 0.8 broadcast_in_dim.5
  64.5 17.6 %all-to-all-start.1 = ((bf16[8,64,328]{2,1,0:T(8,128)(2,1)}), bf16[8,64,328]{2,1,0:T(8,128)(2,1)S(1)}, u32[]{:S(2)}, u32[]{:S(2)}) async-start(bf16[8,64,328]{2,1,0:T(8,128)(2,1)} %broadcast_in_dim.5), calls=%async_computation.1 | async-start | bytes 786432 | tf_op jit(solution)/shard_map/all_to_all | solution.py:252
  82.1 0.6 pad_add_fusion.pos_ref
  82.7 22.4 %factor.1 = (bf16[512,512]{1,0:T(8,128)(2,1)}, bf16[2,256,256]{2,1,0:T(8,128)(2,1)}, bf16[256,256]{1,0:T(8,128)(2,1)}, f32[8,64]{1,0:T(8,128)}) custom-call(s32[2]{0:T(128)} %pad_add_fusion.pos_ref, bf16[4,512,128]{2,1,0:T(8,128)(2,1)} %bitcast.12, bf16[512,512]{1,0:T(8,128)(2,1)} %constant.30.clone.pcol_ref), custom_call_target="tpu_custom_call" | custom-call | tf_op jit(solution)/shard_map/factor/pallas_call | solution.py:209
  105.0 1.1 convolution_convert_fusion.wr_ref
  106.2 0.8 copy-done.3
  107.0 0.3 copy-done.4
  107.3 11.9 %update.1 = f32[328,1,1,2624]{3,2,1,0:T(1,128)} custom-call(s32[2]{0:T(128)} %pad_add_fusion.pos_ref, bf16[512,512]{1,0:T(8,128)(2,1)} %get-tuple-element.12.head_ref, bf16[2,256,256]{2,1,0:T(8,128)(2,1)} %get-tuple-element.13.g_ref, bf16[256,256]{1,0:T(8,128)(2,1)} %get-tuple-element.14.l_ref, f32[8,64]{1,0:T(8,128)} %get-tuple-element.15.own_ref, ...), custom_call_target="tpu_custom_call" | custom-call | tf_op jit(solution)/shard_map/update/pallas_call | solution.py:227
  (27 shorter events, 0.3 us)
Async XLA Ops:
  0.8 24.7 %collective-permute-start.2 = (bf16[8,2688]{1,0:T(8,128)(2,1)S(1)}, bf16[8,2688]{1,0:T(8,128)(2,1)S(1)}, u32[]{:S(2)}, u32[]{:S(2)}) collective-permute-start(bf16[8,2688]{1,0:T(8,128)(2,1)S(1)} %get-tuple-element.17), channel_id=1, source_target_pairs={{0,64},{8,72},{16,80},{24,88},{32,96},{40,104},{48,112},{56,120},{... | collective-permute-start | bytes 129032 | tf_op jit(solution)/shard_map/ppermute | solution.py:256
  16.2 9.2 %collective-permute-start.1 = (bf16[8,2688]{1,0:T(8,128)(2,1)S(1)}, bf16[8,2688]{1,0:T(8,128)(2,1)S(1)}, u32[]{:S(2)}, u32[]{:S(2)}) collective-permute-start(bf16[8,2688]{1,0:T(8,128)(2,1)S(1)} %get-tuple-element.17), channel_id=1, source_target_pairs={{0,96},{8,104},{16,112},{24,120},{32,0},{40,8},{48,16},{56,24},{64... | collective-permute-start | bytes 129032 | tf_op jit(solution)/shard_map/ppermute | solution.py:256
  18.2 9.0 %collective-permute-start = (bf16[8,2688]{1,0:T(8,128)(2,1)S(1)}, bf16[8,2688]{1,0:T(8,128)(2,1)S(1)}, u32[]{:S(2)}, u32[]{:S(2)}) collective-permute-start(bf16[8,2688]{1,0:T(8,128)(2,1)S(1)} %get-tuple-element.17), channel_id=1, source_target_pairs={{0,32},{8,40},{16,48},{24,56},{32,64},{40,72},{48,80},{56,88},{64,... | collective-permute-start | bytes 129032 | tf_op jit(solution)/shard_map/ppermute | solution.py:256
  27.2 15.6 %collective-permute-start.5 = (bf16[32,2688]{1,0:T(8,128)(2,1)S(1)}, bf16[32,2688]{1,0:T(8,128)(2,1)S(1)}, u32[]{:S(2)}, u32[]{:S(2)}) collective-permute-start(bf16[32,2688]{1,0:T(8,128)(2,1)S(1)} %pad_maximum_fusion), channel_id=1, source_target_pairs={{0,16},{8,24},{16,32},{24,40},{32,48},{40,56},{48,64},{56,72},{64,... | collective-permute-start | bytes 516104 | tf_op jit(solution)/shard_map/ppermute | solution.py:256
  32.1 10.7 %collective-permute-start.4 = (bf16[32,2688]{1,0:T(8,128)(2,1)S(1)}, bf16[32,2688]{1,0:T(8,128)(2,1)S(1)}, u32[]{:S(2)}, u32[]{:S(2)}) collective-permute-start(bf16[32,2688]{1,0:T(8,128)(2,1)S(1)} %pad_maximum_fusion), channel_id=1, source_target_pairs={{0,120},{8,0},{16,8},{24,16},{32,24},{40,32},{48,40},{56,48},{64,5... | collective-permute-start | bytes 516104 | tf_op jit(solution)/shard_map/ppermute | solution.py:256
  34.1 8.6 %collective-permute-start.3 = (bf16[32,2688]{1,0:T(8,128)(2,1)S(1)}, bf16[32,2688]{1,0:T(8,128)(2,1)S(1)}, u32[]{:S(2)}, u32[]{:S(2)}) collective-permute-start(bf16[32,2688]{1,0:T(8,128)(2,1)S(1)} %pad_maximum_fusion), channel_id=1, source_target_pairs={{0,8},{8,16},{16,24},{24,32},{32,40},{40,48},{48,56},{56,64},{64,7... | collective-permute-start | bytes 516104 | tf_op jit(solution)/shard_map/ppermute | solution.py:256
  42.8 62.2 %copy-start.2 = (bf16[128,2688]{1,0:T(8,128)(2,1)}, bf16[128,2688]{1,0:T(8,128)(2,1)S(1)}, u32[]{:S(2)}) copy-start(bf16[128,2688]{1,0:T(8,128)(2,1)S(1)} %constant_dynamic-update-slice_fusion.x0_ref) | copy-start | bytes 2064388
  43.9 61.2 %copy-start = (bf16[512,512]{1,0:T(8,128)(2,1)S(1)}, bf16[512,512]{1,0:T(8,128)(2,1)}, u32[]{:S(2)}) copy-start(bf16[512,512]{1,0:T(8,128)(2,1)} %constant.30.clone.pcol_ref) | copy-start | bytes 1572868
  43.9 19.7 %all-to-all-start = ((bf16[32,64,128]{2,1,0:T(8,128)(2,1)}), bf16[32,64,128]{2,1,0:T(8,128)(2,1)S(1)}, u32[]{:S(2)}, u32[]{:S(2)}) async-start(bf16[32,64,128]{2,1,0:T(8,128)(2,1)} %broadcast_in_dim.4), calls=%async_computation | async-start | bytes 1048576 | tf_op jit(solution)/shard_map/all_to_all | solution.py:252
  54.3 51.9 %collective-permute-start.8 = (bf16[128,2688]{1,0:T(8,128)(2,1)S(1)}, bf16[128,2688]{1,0:T(8,128)(2,1)S(1)}, u32[]{:S(2)}, u32[]{:S(2)}) collective-permute-start(bf16[128,2688]{1,0:T(8,128)(2,1)S(1)} %constant_dynamic-update-slice_fusion.x0_ref), channel_id=1, source_target_pairs={{0,256},{128,384},{256,0},{384,128},{1,257},{129,385},{257,1},{385... | collective-permute-start | bytes 2064392 | tf_op jit(solution)/shard_map/ppermute | solution.py:256
  56.5 49.7 %collective-permute-start.7 = (bf16[128,2688]{1,0:T(8,128)(2,1)S(1)}, bf16[128,2688]{1,0:T(8,128)(2,1)S(1)}, u32[]{:S(2)}, u32[]{:S(2)}) collective-permute-start(bf16[128,2688]{1,0:T(8,128)(2,1)S(1)} %constant_dynamic-update-slice_fusion.x0_ref), channel_id=1, source_target_pairs={{0,384},{128,0},{256,128},{384,256},{1,385},{129,1},{257,129},{385... | collective-permute-start | bytes 2064392 | tf_op jit(solution)/shard_map/ppermute | solution.py:256
  60.3 45.9 %collective-permute-start.6 = (bf16[128,2688]{1,0:T(8,128)(2,1)S(1)}, bf16[128,2688]{1,0:T(8,128)(2,1)}, u32[]{:S(2)}, u32[]{:S(2)}) collective-permute-start(bf16[128,2688]{1,0:T(8,128)(2,1)S(1)} %constant_dynamic-update-slice_fusion.x0_ref), channel_id=1, source_target_pairs={{0,128},{128,256},{256,384},{384,0},{1,129},{129,257},{257,385},{3... | collective-permute-start | bytes 2064392 | tf_op jit(solution)/shard_map/ppermute | solution.py:256
  63.5 19.1 %copy-start.1 = (bf16[32,64,128]{2,1,0:T(8,128)(2,1)}, bf16[32,64,128]{2,1,0:T(8,128)(2,1)S(1)}, u32[]{:S(2)}) copy-start(bf16[32,64,128]{2,1,0:T(8,128)(2,1)S(1)} %all-to-all-done) | copy-start | bytes 1572868
  64.5 40.5 %all-to-all-start.1 = ((bf16[8,64,328]{2,1,0:T(8,128)(2,1)}), bf16[8,64,328]{2,1,0:T(8,128)(2,1)S(1)}, u32[]{:S(2)}, u32[]{:S(2)}) async-start(bf16[8,64,328]{2,1,0:T(8,128)(2,1)} %broadcast_in_dim.5), calls=%async_computation.1 | async-start | bytes 786432 | tf_op jit(solution)/shard_map/all_to_all | solution.py:252
  106.2 0.9 copy-start.3
  106.2 1.1 copy-start.4

commit v3 on v2

v3 whole, which is shorter than its diff:
```python
import functools

import jax
import jax.numpy as jnp
import numpy as np
from jax import lax
from jax.experimental import pallas as pl
from jax.experimental.pallas import tpu as pltpu
from jax.sharding import Mesh, PartitionSpec as P

B = 256
STEPS = 2
T = STEPS * B
NB = 64
LANE = 128
WIDE = 16
FAR, NEAR = (4, -4, 8), (1, -1, 2)
NY, NZH, NZL, NX, NC = 4, 4, 4, 4, 2
NZ = NZH * NZL
ROWS, COLS = NY * NZH * NZL, NX * NC
LR, LC = T // ROWS, T // COLS
TILE = 896
HIGH = lax.Precision.HIGHEST
F32, BF16 = jnp.float32, jnp.bfloat16


def mm(a, b, ca=1, cb=0, precision=None):
    return lax.dot_general(
        a, b, (((ca,), (cb,)), ((), ())), precision=precision, preferred_element_type=F32
    )


def eliminate(block):
    row = lax.broadcasted_iota(jnp.int32, (NB, NB), 0)
    col = lax.broadcasted_iota(jnp.int32, (NB, NB), 1)
    eye = (row == col).astype(F32)
    full = jnp.concatenate([block, eye], axis=1)
    groups = NB // 8
    r = [full[8 * g : 8 * g + 8, :] for g in range(groups)]
    sub = lax.broadcasted_iota(jnp.int32, (8, 128), 0)
    scales = [jnp.zeros((8, 128), F32)] * groups
    for b in range(0, NB, WIDE):
        c = [
            {g: jnp.broadcast_to(r[g][:, b + i : b + i + 1], (8, 128)) for g in range(b // 8, groups)}
            for i in range(WIDE)
        ]
        for i in range(0, WIDE, 2):
            top, s = (b + i) // 8, (b + i) % 8
            line = lambda v, k: jnp.broadcast_to(v[k : k + 1, :], (8, 128))
            p, o, q = line(c[i][top], s), line(c[i + 1][top], s), line(c[i + 1][top], s + 1)
            det = p * q - o * o
            inv_p, inv_det = 1.0 / p, 1.0 / det
            tie = o * inv_p
            scales[top] = jnp.where(sub == s, lax.rsqrt(p), jnp.where(sub == s + 1, lax.rsqrt(det * inv_p), scales[top]))
            pd, od, qd = p * inv_det, o * inv_det, q * inv_det
            ahead = {k: (line(c[k][top], s), line(c[k][top], s + 1)) for k in range(i + 2, WIDE)}
            lead = (line(r[top], s), line(r[top], s + 1))
            for g in range(top, groups):
                m1 = c[i][g] * qd - c[i + 1][g] * od
                m2 = c[i + 1][g] * pd - c[i][g] * od
                if g == top:
                    m1 = jnp.where(sub > s + 1, m1, jnp.where(sub == s + 1, tie, 0.0))
                    m2 = jnp.where(sub > s + 1, m2, 0.0)
                for k in range(i + 2, WIDE):
                    c[k][g] = c[k][g] - (m1 * ahead[k][0] + m2 * ahead[k][1])
                r[g] = r[g] - (m1 * lead[0] + m2 * lead[1])
    out = jnp.concatenate([r[g] * scales[g] for g in range(groups)], axis=0)
    upper = jnp.where(row <= col, out[:, :NB], 0.0)
    lower = jnp.where(row >= col, out[:, NB:], 0.0)
    return upper, lower


def factor_panel(a):
    nb = B // NB
    cur = [[a[NB * i : NB * i + NB, NB * j : NB * j + NB] if i >= j else None for j in range(nb)] for i in range(nb)]
    up = [[None] * nb for _ in range(nb)]
    low = [[None] * nb for _ in range(nb)]
    inv = [[None] * nb for _ in range(nb)]
    zero = jnp.zeros((NB, NB), F32)
    for k in range(nb):
        u, g = eliminate(cur[k][k])
        up[k][k] = u
        inv[k][k] = g
        if k + 1 < nb:
            below = jnp.concatenate([cur[i][k] for i in range(k + 1, nb)], axis=0)
            solved = mm(below, g, 1, 1, HIGH)
            for i in range(k + 1, nb):
                low[i][k] = solved[NB * (i - k - 1) : NB * (i - k), :]
            upper = mm(g, below, 1, 1, HIGH)
            for i in range(k + 1, nb):
                up[k][i] = upper[:, NB * (i - k - 1) : NB * (i - k)]
            for j in range(k + 1, nb):
                prod = mm(solved[NB * (j - k - 1) :, :], low[j][k], 1, 1, HIGH)
                for i in range(j, nb):
                    cur[i][j] = cur[i][j] - prod[NB * (i - j) : NB * (i - j + 1), :]
        if k:
            left = jnp.concatenate(low[k][:k], axis=1)
            prev = jnp.concatenate(
                [jnp.concatenate([inv[i][j] if j <= i else zero for j in range(k)], axis=1) for i in range(k)], axis=0
            )
            row = -mm(g, mm(left, prev, 1, 0, HIGH), 1, 0, HIGH)
            for j in range(k):
                inv[k][j] = row[:, NB * j : NB * j + NB]
    upper = jnp.concatenate(
        [jnp.concatenate([up[i][j] if j >= i else zero for j in range(nb)], axis=1) for i in range(nb)], axis=0
    )
    inverse = jnp.concatenate(
        [jnp.concatenate([inv[i][j] if j <= i else zero for j in range(nb)], axis=1) for i in range(nb)], axis=0
    )
    return upper, inverse


def natural_rows(r, absolute):
    stored = lax.broadcasted_iota(jnp.int32, (8, T), 1)

    def shift(place, table):
        code = lax.rem(stored // place, 4)
        out = jnp.zeros_like(code)
        for k, d in enumerate(table):
            out = jnp.where(code == k + 1, d, out)
        return out

    z = lax.rem(lax.rem(r, NZ) - shift(LR, FAR) - shift(4 * LR, NEAR) + 2 * NZ, NZ)
    y = stored // (NZ * LR)
    if not absolute:
        y = lax.rem(r // NZ - shift(NZ * LR, NEAR) + 2 * NY, NY)
    order = lax.rem(stored, LR) * ROWS + y * NZ + z
    return jnp.broadcast_to(order[0:1, :], (B, T))


def factor_kernel(r_ref, q_ref, x_ref, pcol_ref, head_ref, side_ref, g_ref, l_ref, own_ref, u_scr, a_scr):
    r = r_ref[0]
    q = q_ref[0]
    rows = lax.broadcasted_iota(jnp.int32, (B, T), 0)
    order = natural_rows(r, True)
    prow = jnp.concatenate([(rows == order).astype(BF16), (rows + B == order).astype(BF16)], axis=0)
    flat = jnp.concatenate([x_ref[y] for y in range(NY)], axis=1)
    part = mm(pcol_ref[...], flat).astype(BF16)
    a_scr[...] = mm(part, prow, 1, 1)
    order = natural_rows(r, False)
    head_ref[B:T, :] = (rows + B == order).astype(BF16)
    side_ref[B:T, :] = pcol_ref[B:T, :]
    u1, g1 = factor_panel(a_scr[0:B, 0:B])
    g1b = g1.astype(BF16)
    s21 = mm(a_scr[B:T, 0:B].astype(BF16), g1b, 1, 1)
    s21b = s21.astype(BF16)
    a22 = a_scr[B:T, B:T] - mm(s21b, s21b, 1, 1)
    s12 = mm(g1b, a_scr[0:B, B:T].astype(BF16), 1, 0)
    l_ref[...] = s21b
    head_ref[0:B, :] = mm(g1b, (rows == order).astype(BF16)).astype(BF16)
    side_ref[0:B, :] = mm(g1b, pcol_ref[0:B, :]).astype(BF16)
    for k in range(B // LANE):
        lanes = slice(LANE * k, LANE * k + LANE)
        u_scr[k, 0:B, :] = u1.T[:, lanes]
        u_scr[k, B:T, :] = s21[:, lanes]
        u_scr[B // LANE + k, 0:B, :] = s12[:, lanes]
    pick = (
        lax.broadcasted_iota(jnp.int32, (T, LC), 0) == lax.broadcasted_iota(jnp.int32, (T, LC), 1) * COLS + q
    ).astype(F32)
    u2, g2 = factor_panel(a22)
    g_ref[...] = g2.astype(BF16)
    for k in range(B // LANE):
        u_scr[B // LANE + k, B:T, :] = u2.T[:, LANE * k : LANE * k + LANE]
    own = jnp.concatenate([u_scr[k, pl.ds(r, LR, stride=ROWS), :] for k in range(T // LANE)], axis=1)
    own_ref[...] = mm(own, pick, 1, 0, HIGH)


def update_kernel(
    r_ref, q_ref, head_ref, side_ref, g_ref, l_ref, own_ref, wr_ref, x0_ref, x1_ref, x2_ref, x3_ref, w_ref, out_ref,
    x_scr, w_scr, out_scr, s_scr, u_scr, x_sem, w_sem, out_sem,
):
    rows, cols = w_ref.shape
    spans = [(lo, min(TILE, cols - lo)) for lo in range(0, cols, TILE)]
    pieces = (x0_ref, x1_ref, x2_ref, x3_ref)
    x_copies = [
        [
            pltpu.make_async_copy(
                ref.at[:, pl.ds(lo, TILE)], x_scr.at[n, pl.ds(T // NY * k, T // NY), :], x_sem.at[n, k]
            )
            for k, ref in enumerate(pieces)
        ]
        for n, (lo, _) in enumerate(spans)
    ]
    w_copy = pltpu.make_async_copy(w_ref, w_scr, w_sem)
    for copy in x_copies[0]:
        copy.start()
    w_copy.start()
    for copies in x_copies[1:]:
        for copy in copies:
            copy.start()

    r, q = r_ref[0], q_ref[0]
    l21 = l_ref[...]
    g2 = g_ref[...]

    def solve(head, panel):
        both = mm(head, panel)
        u1 = both[0:B, :]
        u1b = u1.astype(BF16)
        c2 = (both[B:T, :] - mm(l21, u1b)).astype(BF16)
        u2 = mm(g2, c2)
        return u1, u2, jnp.concatenate([u1b, u2.astype(BF16)], axis=0)

    s1, s2, sb = solve(side_ref[...], wr_ref[...])
    srow = sb.T
    width = pl.cdiv(rows, LANE)
    for k in range(width):
        lanes = min(LANE, rows - LANE * k)
        s_scr[k, 0:B, 0:lanes] = s1[:, LANE * k : LANE * k + lanes]
        s_scr[k, B:T, 0:lanes] = s2[:, LANE * k : LANE * k + lanes]
    mine = jnp.concatenate([s_scr[k, pl.ds(q, LC, stride=COLS), :] for k in range(width)], axis=1)
    scol = mine.T[0:rows, :]

    out_copies = []
    for n, (lo, size) in enumerate(spans):
        for copy in x_copies[n]:
            copy.wait()
        u1, u2, ub = solve(head_ref[...], x_scr[n])
        for k in range(TILE // LANE):
            u_scr[k, 0:B, :] = u1[:, LANE * k : LANE * k + LANE]
            u_scr[k, B:T, :] = u2[:, LANE * k : LANE * k + LANE]
        if n == 0:
            w_copy.wait()
        done = mm(srow, ub)[:, 0:size]
        out_scr[:, 0, 0, lo : lo + size] = w_scr[:, lo : lo + size].astype(F32) - done
        for k in range(TILE // LANE):
            lanes = min(LANE, size - LANE * k)
            line = u_scr[k, pl.ds(r, LR, stride=ROWS), :]
            out_scr[0:LR, 0, 0, lo + LANE * k : lo + LANE * k + lanes] = line[:, 0:lanes]
        if n == 0:
            out_scr[:, 0, 0, 0:LC] = scol
            out_scr[0:LR, 0, 0, 0:LC] = own_ref[...]
        copy = pltpu.make_async_copy(
            out_scr.at[:, :, :, pl.ds(lo, size)], out_ref.at[:, :, :, pl.ds(lo, size)], out_sem.at[n]
        )
        copy.start()
        out_copies.append(copy)
    for copy in out_copies:
        copy.wait()


def column_order():
    nat = np.arange(T)
    pcol = np.zeros((T, T), np.float32)
    pcol[nat, (nat % COLS) * LC + nat // COLS] = 1
    return pcol.astype(jnp.bfloat16)


def factor(pos, corner, pcol):
    vmem = pl.BlockSpec(memory_space=pltpu.VMEM)
    return pl.pallas_call(
        factor_kernel,
        out_shape=(
            jax.ShapeDtypeStruct((T, T), BF16),
            jax.ShapeDtypeStruct((T, T), BF16),
            jax.ShapeDtypeStruct((B, B), BF16),
            jax.ShapeDtypeStruct((B, B), BF16),
            jax.ShapeDtypeStruct((LR, LC), F32),
        ),
        in_specs=[pl.BlockSpec(memory_space=pltpu.SMEM)] * 2 + [vmem] * 2,
        out_specs=(vmem,) * 5,
        scratch_shapes=[pltpu.VMEM((T // LANE, T, LANE), F32), pltpu.VMEM((T, T), F32)],
        cost_estimate=pl.CostEstimate(flops=40_000_000_000, transcendentals=0, bytes_accessed=4 * T * T),
        name="factor",
    )(*pos, corner, pcol)


def update(pos, head, side, g2, l21, own, wr, xs, w):
    rows, cols = w.shape
    steps = pl.cdiv(cols, TILE)
    whole = lambda a: pl.BlockSpec(a.shape, lambda i: (0,) * a.ndim)
    hbm = pl.BlockSpec(memory_space=pl.ANY)
    return pl.pallas_call(
        update_kernel,
        grid=(1,),
        out_shape=jax.ShapeDtypeStruct((rows, 1, 1, cols), F32),
        in_specs=[pl.BlockSpec(memory_space=pltpu.SMEM)] * 2
        + [whole(a) for a in (head, side, g2, l21, own, wr)]
        + [hbm] * (NY + 1),
        out_specs=hbm,
        scratch_shapes=[
            pltpu.VMEM((steps, T, TILE), BF16),
            pltpu.VMEM((rows, cols), BF16),
            pltpu.VMEM((rows, 1, 1, cols), F32),
            pltpu.VMEM((pl.cdiv(rows, LANE), T, LANE), F32),
            pltpu.VMEM((TILE // LANE, T, LANE), F32),
            pltpu.SemaphoreType.DMA((steps, NY)),
            pltpu.SemaphoreType.DMA,
            pltpu.SemaphoreType.DMA((steps,)),
        ],
        name="update",
    )(*pos, head, side, g2, l21, own, wr, *xs, w)


def everyone(x, axis, count):
    return lax.all_to_all(jnp.broadcast_to(x[None], (count,) + x.shape), axis, 0, 0, tiled=True)


def spread(x, axis, count, shifts):
    parts = [lax.ppermute(x, axis, [(i, (i + d) % count) for i in range(count)]) for d in shifts]
    return [x] + parts


def on_device(kernel):
    work = kernel[:, 0, 0, :]
    rows, cols = work.shape
    r = lax.axis_index(("y", "zh", "zl"))
    q = lax.axis_index(("x", "c"))
    pos = (r.reshape(1).astype(jnp.int32), q.reshape(1).astype(jnp.int32))
    pcol = jnp.asarray(column_order())
    head_rows = jnp.pad(work[0:LR, :], ((0, 0), (0, -cols % LANE)))

    wr = everyone(jnp.transpose(work[:, 0:LC]), ("x", "c"), COLS).reshape(T, rows)

    x = jnp.concatenate(spread(head_rows, ("zh", "zl"), NZ, FAR), axis=0)
    x = jnp.concatenate(spread(x, ("zh", "zl"), NZ, NEAR), axis=0)
    x, wr = lax.optimization_barrier((x, wr))
    pieces = jnp.broadcast_to(jnp.transpose(x[:, 0:LC])[None], (NY * COLS, LC, NZ * LR))
    x, pieces = lax.optimization_barrier((x, pieces))
    corner = lax.all_to_all(pieces, ("y", "x", "c"), 0, 0, tiled=True).reshape(NY, T, NZ * LR)
    xs = spread(x, "y", NY, NEAR)

    head, side, g2, l21, own = factor(pos, corner, pcol)
    return update(pos, head, side, g2, l21, own, wr, xs, work)


def solution(mesh):
    inner = Mesh(mesh.devices.reshape(NY, NZH, NZL, NX, NC), ("y", "zh", "zl", "x", "c"))
    spec = P(None, ("y", "zh", "zl"), ("x", "c"), None)
    return jax.shard_map(on_device, mesh=inner, in_specs=(spec,), out_specs=spec, check_vma=False)
```

time: 120 us -> 112 us (0.933)
  the two profiles are of different devices: /device:TPU:19 before, /device:TPU:20 now
where the time goes in v3:
time: 112 us; the launch traced here: 111 us
  starting transfers between devices  55.6 us (50%)
  Pallas kernels  28.6 us (26%)
  waiting for transfers between devices  21.5 us (19%)
  local copies, waits for them, and re-layouts  5.07 us (5%)
    ppermute x9, starting transfers between devices, spread(): lax.ppermute(x, axis, [(i, (i + d) % count) for i in range(count)])  43.3 us
    pallas_call x1, Pallas kernels, factor(): pl.pallas_call(factor_kernel, out_shape=(jax.ShapeDtypeStruct((T, T), BF1...  19.8 us
    all_to_all x1, waiting for transfers between devices, on_device(): lax.all_to_all(pieces, ('y', 'x', 'c'), 0, 0, tiled=True)  13.6 us
    pallas_call x1, Pallas kernels, update(): pl.pallas_call(update_kernel, grid=(1,), out_shape=jax.ShapeDtypeStruct((...  8.83 us
    ppermute x9, waiting for transfers between devices, spread(): lax.ppermute(x, axis, [(i, (i + d) % count) for i in range(count)])  7.89 us
    all_to_all x1, starting transfers between devices, on_device(): lax.all_to_all(pieces, ('y', 'x', 'c'), 0, 0, tiled=True)  7.44 us
    all_to_all x1, starting transfers between devices, everyone(): lax.all_to_all(jnp.broadcast_to(x[None], (count,) + x.shape), axis, 0, 0,...  4.8 us
  transfers between devices with their start and end apart: 11, of which 2 were waited for; matrix products, arithmetic and copies ran while one was open for 2% of the time, Pallas kernels for 18%

profile of v3, /device:TPU:20, one launch (start us, length us, event | category | flops | bytes accessed | tf_op | source)
XLA Modules:
  0.0 111.2 jit_solution(9824286713998155633)
XLA Ops:
  0.0 0.8 slice_bitcast_fusion.1
  0.8 15.7 %collective-permute-start.2 = (bf16[8,2688]{1,0:T(8,128)(2,1)S(1)}, bf16[8,2688]{1,0:T(8,128)(2,1)S(1)}, u32[]{:S(2)}, u32[]{:S(2)}) collective-permute-start(bf16[8,2688]{1,0:T(8,128)(2,1)S(1)} %get-tuple-element.23), channel_id=1, source_target_pairs={{0,64},{8,72},{16,80},{24,88},{32,96},{40,104},{48,112},{56,120},{... | collective-permute-start | bytes 129032 | tf_op jit(solution)/shard_map/ppermute | solution.py:300
  16.5 1.9 %collective-permute-start.1 = (bf16[8,2688]{1,0:T(8,128)(2,1)S(1)}, bf16[8,2688]{1,0:T(8,128)(2,1)S(1)}, u32[]{:S(2)}, u32[]{:S(2)}) collective-permute-start(bf16[8,2688]{1,0:T(8,128)(2,1)S(1)} %get-tuple-element.23), channel_id=1, source_target_pairs={{0,96},{8,104},{16,112},{24,120},{32,0},{40,8},{48,16},{56,24},{64... | collective-permute-start | bytes 129032 | tf_op jit(solution)/shard_map/ppermute | solution.py:300
  18.5 7.8 %collective-permute-start = (bf16[8,2688]{1,0:T(8,128)(2,1)S(1)}, bf16[8,2688]{1,0:T(8,128)(2,1)S(1)}, u32[]{:S(2)}, u32[]{:S(2)}) collective-permute-start(bf16[8,2688]{1,0:T(8,128)(2,1)S(1)} %get-tuple-element.23), channel_id=1, source_target_pairs={{0,32},{8,40},{16,48},{24,56},{32,64},{40,72},{48,80},{56,88},{64,... | collective-permute-start | bytes 129032 | tf_op jit(solution)/shard_map/ppermute | solution.py:300
  26.3 0.9 slice_bitcast_fusion
  27.2 0.1 copy.3
  27.3 0.8 broadcast_in_dim.4
  28.1 4.8 %all-to-all-start = ((bf16[8,64,328]{2,1,0:T(8,128)(2,1)}), bf16[8,64,328]{2,1,0:T(8,128)(2,1)S(1)}, u32[]{:S(2)}, u32[]{:S(2)}) async-start(bf16[8,64,328]{2,1,0:T(8,128)(2,1)} %broadcast_in_dim.4), calls=%async_computation | async-start | bytes 786432 | tf_op jit(solution)/shard_map/all_to_all | solution.py:296
  32.9 3.4 %collective-permute-start.5 = (bf16[32,2688]{1,0:T(8,128)(2,1)S(1)}, bf16[32,2688]{1,0:T(8,128)(2,1)S(1)}, u32[]{:S(2)}, u32[]{:S(2)}) collective-permute-start(bf16[32,2688]{1,0:T(8,128)(2,1)S(1)} %pad_maximum_fusion), channel_id=1, source_target_pairs={{0,16},{8,24},{16,32},{24,40},{32,48},{40,56},{48,64},{56,72},{64,... | collective-permute-start | bytes 516104 | tf_op jit(solution)/shard_map/ppermute | solution.py:300
  36.3 4.1 %collective-permute-start.4 = (bf16[32,2688]{1,0:T(8,128)(2,1)S(1)}, bf16[32,2688]{1,0:T(8,128)(2,1)S(1)}, u32[]{:S(2)}, u32[]{:S(2)}) collective-permute-start(bf16[32,2688]{1,0:T(8,128)(2,1)S(1)} %pad_maximum_fusion), channel_id=1, source_target_pairs={{0,120},{8,0},{16,8},{24,16},{32,24},{40,32},{48,40},{56,48},{64,5... | collective-permute-start | bytes 516104 | tf_op jit(solution)/shard_map/ppermute | solution.py:300
  40.5 1.9 %collective-permute-start.3 = (bf16[32,2688]{1,0:T(8,128)(2,1)S(1)}, bf16[32,2688]{1,0:T(8,128)(2,1)S(1)}, u32[]{:S(2)}, u32[]{:S(2)}) collective-permute-start(bf16[32,2688]{1,0:T(8,128)(2,1)S(1)} %pad_maximum_fusion), channel_id=1, source_target_pairs={{0,8},{8,16},{16,24},{24,32},{32,40},{40,48},{48,56},{56,64},{64,7... | collective-permute-start | bytes 516104 | tf_op jit(solution)/shard_map/ppermute | solution.py:300
  42.4 7.9 %collective-permute-done.3 = bf16[32,2688]{1,0:T(8,128)(2,1)S(1)} collective-permute-done((bf16[32,2688]{1,0:T(8,128)(2,1)S(1)}, bf16[32,2688]{1,0:T(8,128)(2,1)S(1)}, u32[]{:S(2)}, u32[]{:S(2)}) %collective-permute-start.3) | collective-permute-done | bytes 172064 | tf_op jit(solution)/shard_map/ppermute | solution.py:300
  50.4 0.1 copy.4
  50.5 1.0 broadcast_in_dim.5
  51.5 7.4 %all-to-all-start.1 = ((bf16[32,64,128]{2,1,0:T(8,128)(2,1)}), bf16[32,64,128]{2,1,0:T(8,128)(2,1)}, u32[]{:S(2)}, u32[]{:S(2)}) async-start(bf16[32,64,128]{2,1,0:T(8,128)(2,1)} %broadcast_in_dim.5), calls=%async_computation.1 | async-start | bytes 1048576 | tf_op jit(solution)/shard_map/all_to_all | solution.py:320
  59.0 2.5 %collective-permute-start.8 = (bf16[128,2688]{1,0:T(8,128)(2,1)S(1)}, bf16[128,2688]{1,0:T(8,128)(2,1)S(1)}, u32[]{:S(2)}, u32[]{:S(2)}) collective-permute-start(bf16[128,2688]{1,0:T(8,128)(2,1)S(1)} %constant_dynamic-update-slice_fusion.x0_ref), channel_id=1, source_target_pairs={{0,256},{128,384},{256,0},{384,128},{1,257},{129,385},{257,1},{385... | collective-permute-start | bytes 2064392 | tf_op jit(solution)/shard_map/ppermute | solution.py:300
  61.5 4.0 %collective-permute-start.7 = (bf16[128,2688]{1,0:T(8,128)(2,1)S(1)}, bf16[128,2688]{1,0:T(8,128)(2,1)S(1)}, u32[]{:S(2)}, u32[]{:S(2)}) collective-permute-start(bf16[128,2688]{1,0:T(8,128)(2,1)S(1)} %constant_dynamic-update-slice_fusion.x0_ref), channel_id=1, source_target_pairs={{0,384},{128,0},{256,128},{384,256},{1,385},{129,1},{257,129},{385... | collective-permute-start | bytes 2064392 | tf_op jit(solution)/shard_map/ppermute | solution.py:300
  65.5 1.9 %collective-permute-start.6 = (bf16[128,2688]{1,0:T(8,128)(2,1)S(1)}, bf16[128,2688]{1,0:T(8,128)(2,1)S(1)}, u32[]{:S(2)}, u32[]{:S(2)}) collective-permute-start(bf16[128,2688]{1,0:T(8,128)(2,1)S(1)} %constant_dynamic-update-slice_fusion.x0_ref), channel_id=1, source_target_pairs={{0,128},{128,256},{256,384},{384,0},{1,129},{129,257},{257,385},{3... | collective-permute-start | bytes 2064392 | tf_op jit(solution)/shard_map/ppermute | solution.py:300
  67.4 13.6 %all-to-all-done.1 = bf16[32,64,128]{2,1,0:T(8,128)(2,1)} async-done(((bf16[32,64,128]{2,1,0:T(8,128)(2,1)}), bf16[32,64,128]{2,1,0:T(8,128)(2,1)}, u32[]{:S(2)}, u32[]{:S(2)}) %all-to-all-start.1) | async-done | bytes 524320 | tf_op jit(solution)/shard_map/all_to_all | solution.py:320
  81.1 19.8 %factor.1 = (bf16[512,512]{1,0:T(8,128)(2,1)}, bf16[512,512]{1,0:T(8,128)(2,1)}, bf16[256,256]{1,0:T(8,128)(2,1)}, bf16[256,256]{1,0:T(8,128)(2,1)}, f32[8,64]{1,0:T(8,128)}) custom-call(s32[1]{0:T(128)} %bitcast.r_ref, s32[1]{0:T(128)} %bitcast.1.q_ref, bf16[4,512,128]{2,1,0:T(8,128)(2,1)} %bitcast.7.x_ref, bf16[512,512]{1,0:T(8,128)(2,1)} %constant.30.clone.pcol_ref), custom_call_target="tpu_custom_call" | custom-call | flops 40000000000 | bytes 1048576 | tf_op jit(solution)/shard_map/factor/pallas_call | solution.py:251
  100.9 0.8 copy-done.2
  101.7 0.3 copy-done.3
  102.0 0.2 copy-done.4
  102.2 8.8 %update.1 = f32[328,1,1,2624]{3,2,1,0:T(1,128)} custom-call(s32[1]{0:T(128)} %bitcast.r_ref, s32[1]{0:T(128)} %bitcast.1.q_ref, bf16[512,512]{1,0:T(8,128)(2,1)} %get-tuple-element.16.head_ref, bf16[512,512]{1,0:T(8,128)(2,1)} %get-tuple-element.17.side_ref, bf16[256,256]{1,0:T(8,128)(2,1)} %get-tuple-element.18.g_ref, ...), custom_call_target="tpu_custom_call" | custom-call | tf_op jit(solution)/shard_map/update/pallas_call | solution.py:273
  (25 shorter events, 0.2 us)
Async XLA Ops:
  0.8 32.1 %collective-permute-start.2 = (bf16[8,2688]{1,0:T(8,128)(2,1)S(1)}, bf16[8,2688]{1,0:T(8,128)(2,1)S(1)}, u32[]{:S(2)}, u32[]{:S(2)}) collective-permute-start(bf16[8,2688]{1,0:T(8,128)(2,1)S(1)} %get-tuple-element.23), channel_id=1, source_target_pairs={{0,64},{8,72},{16,80},{24,88},{32,96},{40,104},{48,112},{56,120},{... | collective-permute-start | bytes 129032 | tf_op jit(solution)/shard_map/ppermute | solution.py:300
  16.5 16.4 %collective-permute-start.1 = (bf16[8,2688]{1,0:T(8,128)(2,1)S(1)}, bf16[8,2688]{1,0:T(8,128)(2,1)S(1)}, u32[]{:S(2)}, u32[]{:S(2)}) collective-permute-start(bf16[8,2688]{1,0:T(8,128)(2,1)S(1)} %get-tuple-element.23), channel_id=1, source_target_pairs={{0,96},{8,104},{16,112},{24,120},{32,0},{40,8},{48,16},{56,24},{64... | collective-permute-start | bytes 129032 | tf_op jit(solution)/shard_map/ppermute | solution.py:300
  18.5 14.4 %collective-permute-start = (bf16[8,2688]{1,0:T(8,128)(2,1)S(1)}, bf16[8,2688]{1,0:T(8,128)(2,1)S(1)}, u32[]{:S(2)}, u32[]{:S(2)}) collective-permute-start(bf16[8,2688]{1,0:T(8,128)(2,1)S(1)} %get-tuple-element.23), channel_id=1, source_target_pairs={{0,32},{8,40},{16,48},{24,56},{32,64},{40,72},{48,80},{56,88},{64,... | collective-permute-start | bytes 129032 | tf_op jit(solution)/shard_map/ppermute | solution.py:300
  28.1 22.3 %all-to-all-start = ((bf16[8,64,328]{2,1,0:T(8,128)(2,1)}), bf16[8,64,328]{2,1,0:T(8,128)(2,1)S(1)}, u32[]{:S(2)}, u32[]{:S(2)}) async-start(bf16[8,64,328]{2,1,0:T(8,128)(2,1)} %broadcast_in_dim.4), calls=%async_computation | async-start | bytes 786432 | tf_op jit(solution)/shard_map/all_to_all | solution.py:296
  32.9 17.4 %collective-permute-start.5 = (bf16[32,2688]{1,0:T(8,128)(2,1)S(1)}, bf16[32,2688]{1,0:T(8,128)(2,1)S(1)}, u32[]{:S(2)}, u32[]{:S(2)}) collective-permute-start(bf16[32,2688]{1,0:T(8,128)(2,1)S(1)} %pad_maximum_fusion), channel_id=1, source_target_pairs={{0,16},{8,24},{16,32},{24,40},{32,48},{40,56},{48,64},{56,72},{64,... | collective-permute-start | bytes 516104 | tf_op jit(solution)/shard_map/ppermute | solution.py:300
  36.3 14.0 %collective-permute-start.4 = (bf16[32,2688]{1,0:T(8,128)(2,1)S(1)}, bf16[32,2688]{1,0:T(8,128)(2,1)S(1)}, u32[]{:S(2)}, u32[]{:S(2)}) collective-permute-start(bf16[32,2688]{1,0:T(8,128)(2,1)S(1)} %pad_maximum_fusion), channel_id=1, source_target_pairs={{0,120},{8,0},{16,8},{24,16},{32,24},{40,32},{48,40},{56,48},{64,5... | collective-permute-start | bytes 516104 | tf_op jit(solution)/shard_map/ppermute | solution.py:300
  40.5 9.8 %collective-permute-start.3 = (bf16[32,2688]{1,0:T(8,128)(2,1)S(1)}, bf16[32,2688]{1,0:T(8,128)(2,1)S(1)}, u32[]{:S(2)}, u32[]{:S(2)}) collective-permute-start(bf16[32,2688]{1,0:T(8,128)(2,1)S(1)} %pad_maximum_fusion), channel_id=1, source_target_pairs={{0,8},{8,16},{16,24},{24,32},{32,40},{40,48},{48,56},{56,64},{64,7... | collective-permute-start | bytes 516104 | tf_op jit(solution)/shard_map/ppermute | solution.py:300
  50.4 50.5 %copy-start.1 = (bf16[128,2688]{1,0:T(8,128)(2,1)}, bf16[128,2688]{1,0:T(8,128)(2,1)S(1)}, u32[]{:S(2)}) copy-start(bf16[128,2688]{1,0:T(8,128)(2,1)S(1)} %constant_dynamic-update-slice_fusion.x0_ref) | copy-start | bytes 2064388
  50.4 50.5 %copy-start = (bf16[8,64,328]{2,1,0:T(8,128)(2,1)}, bf16[8,64,328]{2,1,0:T(8,128)(2,1)S(1)}, u32[]{:S(2)}) copy-start(bf16[8,64,328]{2,1,0:T(8,128)(2,1)S(1)} %all-to-all-done) | copy-start | bytes 1007620
  51.5 29.5 %all-to-all-start.1 = ((bf16[32,64,128]{2,1,0:T(8,128)(2,1)}), bf16[32,64,128]{2,1,0:T(8,128)(2,1)}, u32[]{:S(2)}, u32[]{:S(2)}) async-start(bf16[32,64,128]{2,1,0:T(8,128)(2,1)} %broadcast_in_dim.5), calls=%async_computation.1 | async-start | bytes 1048576 | tf_op jit(solution)/shard_map/all_to_all | solution.py:320
  59.0 41.9 %collective-permute-start.8 = (bf16[128,2688]{1,0:T(8,128)(2,1)S(1)}, bf16[128,2688]{1,0:T(8,128)(2,1)S(1)}, u32[]{:S(2)}, u32[]{:S(2)}) collective-permute-start(bf16[128,2688]{1,0:T(8,128)(2,1)S(1)} %constant_dynamic-update-slice_fusion.x0_ref), channel_id=1, source_target_pairs={{0,256},{128,384},{256,0},{384,128},{1,257},{129,385},{257,1},{385... | collective-permute-start | bytes 2064392 | tf_op jit(solution)/shard_map/ppermute | solution.py:300
  61.5 39.4 %collective-permute-start.7 = (bf16[128,2688]{1,0:T(8,128)(2,1)S(1)}, bf16[128,2688]{1,0:T(8,128)(2,1)S(1)}, u32[]{:S(2)}, u32[]{:S(2)}) collective-permute-start(bf16[128,2688]{1,0:T(8,128)(2,1)S(1)} %constant_dynamic-update-slice_fusion.x0_ref), channel_id=1, source_target_pairs={{0,384},{128,0},{256,128},{384,256},{1,385},{129,1},{257,129},{385... | collective-permute-start | bytes 2064392 | tf_op jit(solution)/shard_map/ppermute | solution.py:300
  65.5 35.4 %collective-permute-start.6 = (bf16[128,2688]{1,0:T(8,128)(2,1)S(1)}, bf16[128,2688]{1,0:T(8,128)(2,1)S(1)}, u32[]{:S(2)}, u32[]{:S(2)}) collective-permute-start(bf16[128,2688]{1,0:T(8,128)(2,1)S(1)} %constant_dynamic-update-slice_fusion.x0_ref), channel_id=1, source_target_pairs={{0,128},{128,256},{256,384},{384,0},{1,129},{129,257},{257,385},{3... | collective-permute-start | bytes 2064392 | tf_op jit(solution)/shard_map/ppermute | solution.py:300
  100.9 0.9 copy-start.2
  100.9 1.1 copy-start.3
  100.9 1.3 %copy-start.4 = (bf16[128,2688]{1,0:T(8,128)(2,1)}, bf16[128,2688]{1,0:T(8,128)(2,1)S(1)}, u32[]{:S(2)}) copy-start(bf16[128,2688]{1,0:T(8,128)(2,1)S(1)} %collective-permute-done.6.x1_ref) | copy-start | bytes 2064388

commit v4 on v3

--- a/solution.py
+++ b/solution.py
@@ -166,16 +166,18 @@
 
 
 def update_kernel(
-    r_ref, q_ref, head_ref, side_ref, g_ref, l_ref, own_ref, wr_ref, x0_ref, x1_ref, x2_ref, x3_ref, w_ref, out_ref,
+    r_ref, q_ref, head_ref, side_ref, g_ref, l_ref, own_ref, wr_ref,
+    x0_ref, x1_ref, x2_ref, x3_ref, x4_ref, x5_ref, x6_ref, w_ref, out_ref,
     x_scr, w_scr, out_scr, s_scr, u_scr, x_sem, w_sem, out_sem,
 ):
     rows, cols = w_ref.shape
     spans = [(lo, min(TILE, cols - lo)) for lo in range(0, cols, TILE)]
-    pieces = (x0_ref, x1_ref, x2_ref, x3_ref)
+    pieces = (x0_ref, x1_ref, x2_ref, x3_ref, x4_ref, x5_ref, x6_ref)
+    starts = [sum(ref.shape[0] for ref in pieces[:k]) for k in range(len(pieces))]
     x_copies = [
         [
             pltpu.make_async_copy(
-                ref.at[:, pl.ds(lo, TILE)], x_scr.at[n, pl.ds(T // NY * k, T // NY), :], x_sem.at[n, k]
+                ref.at[:, pl.ds(lo, TILE)], x_scr.at[n, pl.ds(starts[k], ref.shape[0]), :], x_sem.at[n, k]
             )
             for k, ref in enumerate(pieces)
         ]
@@ -261,6 +263,7 @@
         out_specs=(vmem,) * 5,
         scratch_shapes=[pltpu.VMEM((T // LANE, T, LANE), F32), pltpu.VMEM((T, T), F32)],
         cost_estimate=pl.CostEstimate(flops=40_000_000_000, transcendentals=0, bytes_accessed=4 * T * T),
+        compiler_params=pltpu.CompilerParams(vmem_limit_bytes=24 << 20),
         name="factor",
     )(*pos, corner, pcol)
 
@@ -276,7 +279,7 @@
         out_shape=jax.ShapeDtypeStruct((rows, 1, 1, cols), F32),
         in_specs=[pl.BlockSpec(memory_space=pltpu.SMEM)] * 2
         + [whole(a) for a in (head, side, g2, l21, own, wr)]
-        + [hbm] * (NY + 1),
+        + [hbm] * (len(xs) + 1),
         out_specs=hbm,
         scratch_shapes=[
             pltpu.VMEM((steps, T, TILE), BF16),
@@ -284,10 +287,11 @@
             pltpu.VMEM((rows, 1, 1, cols), F32),
             pltpu.VMEM((pl.cdiv(rows, LANE), T, LANE), F32),
             pltpu.VMEM((TILE // LANE, T, LANE), F32),
-            pltpu.SemaphoreType.DMA((steps, NY)),
+            pltpu.SemaphoreType.DMA((steps, len(xs))),
             pltpu.SemaphoreType.DMA,
             pltpu.SemaphoreType.DMA((steps,)),
         ],
+        compiler_params=pltpu.CompilerParams(vmem_limit_bytes=32 << 20),
         name="update",
     )(*pos, head, side, g2, l21, own, wr, *xs, w)
 
@@ -313,12 +317,13 @@
     wr = everyone(jnp.transpose(work[:, 0:LC]), ("x", "c"), COLS).reshape(T, rows)
 
     x = jnp.concatenate(spread(head_rows, ("zh", "zl"), NZ, FAR), axis=0)
+    across = spread(x, "y", NY, NEAR[2:])[1]
     x = jnp.concatenate(spread(x, ("zh", "zl"), NZ, NEAR), axis=0)
     x, wr = lax.optimization_barrier((x, wr))
     pieces = jnp.broadcast_to(jnp.transpose(x[:, 0:LC])[None], (NY * COLS, LC, NZ * LR))
-    x, pieces = lax.optimization_barrier((x, pieces))
+    x, across, pieces = lax.optimization_barrier((x, across, pieces))
     corner = lax.all_to_all(pieces, ("y", "x", "c"), 0, 0, tiled=True).reshape(NY, T, NZ * LR)
-    xs = spread(x, "y", NY, NEAR)
+    xs = spread(x, "y", NY, NEAR[:2]) + spread(across, ("zh", "zl"), NZ, NEAR)
 
     head, side, g2, l21, own = factor(pos, corner, pcol)
     return update(pos, head, side, g2, l21, own, wr, xs, work)

time: 112 us -> 105 us (0.938)
  the two profiles are of different devices: /device:TPU:20 before, /device:TPU:1 now
where the time goes in v4:
time: 105 us; the launch traced here: 104 us
  starting transfers between devices  65.3 us (62%)
  Pallas kernels  25.7 us (24%)
  waiting for transfers between devices  7.88 us (8%)
  local copies, waits for them, and re-layouts  4.72 us (4%)
    ppermute x12, starting transfers between devices, spread(): lax.ppermute(x, axis, [(i, (i + d) % count) for i in range(count)])  53.4 us
    pallas_call x1, Pallas kernels, factor(): pl.pallas_call(factor_kernel, out_shape=(jax.ShapeDtypeStruct((T, T), BF1...  17.9 us
    ppermute x12, waiting for transfers between devices, spread(): lax.ppermute(x, axis, [(i, (i + d) % count) for i in range(count)])  7.88 us
    pallas_call x1, Pallas kernels, update(): pl.pallas_call(update_kernel, grid=(1,), out_shape=jax.ShapeDtypeStruct((...  7.8 us
    all_to_all x1, starting transfers between devices, on_device(): lax.all_to_all(pieces, ('y', 'x', 'c'), 0, 0, tiled=True)  6.06 us
    all_to_all x1, starting transfers between devices, everyone(): lax.all_to_all(jnp.broadcast_to(x[None], (count,) + x.shape), axis, 0, 0,...  5.81 us
  transfers between devices with their start and end apart: 14, of which 1 were waited for; matrix products, arithmetic and copies ran while one was open for 2% of the time, Pallas kernels for 17%

profile of v4, /device:TPU:1, one launch (start us, length us, event | category | flops | bytes accessed | tf_op | source)
XLA Modules:
  0.0 104.0 jit_solution(1139205964461978899)
XLA Ops:
  0.0 0.8 slice_bitcast_fusion.1
  0.8 16.3 %collective-permute-start.2 = (bf16[8,2688]{1,0:T(8,128)(2,1)S(1)}, bf16[8,2688]{1,0:T(8,128)(2,1)S(1)}, u32[]{:S(2)}, u32[]{:S(2)}) collective-permute-start(bf16[8,2688]{1,0:T(8,128)(2,1)S(1)} %get-tuple-element.25), channel_id=1, source_target_pairs={{0,64},{8,72},{16,80},{24,88},{32,96},{40,104},{48,112},{56,120},{... | collective-permute-start | bytes 129032 | tf_op jit(solution)/shard_map/ppermute | solution.py:304
  17.1 1.9 %collective-permute-start.1 = (bf16[8,2688]{1,0:T(8,128)(2,1)S(1)}, bf16[8,2688]{1,0:T(8,128)(2,1)S(1)}, u32[]{:S(2)}, u32[]{:S(2)}) collective-permute-start(bf16[8,2688]{1,0:T(8,128)(2,1)S(1)} %get-tuple-element.25), channel_id=1, source_target_pairs={{0,96},{8,104},{16,112},{24,120},{32,0},{40,8},{48,16},{56,24},{64... | collective-permute-start | bytes 129032 | tf_op jit(solution)/shard_map/ppermute | solution.py:304
  19.0 7.3 %collective-permute-start = (bf16[8,2688]{1,0:T(8,128)(2,1)S(1)}, bf16[8,2688]{1,0:T(8,128)(2,1)S(1)}, u32[]{:S(2)}, u32[]{:S(2)}) collective-permute-start(bf16[8,2688]{1,0:T(8,128)(2,1)S(1)} %get-tuple-element.25), channel_id=1, source_target_pairs={{0,32},{8,40},{16,48},{24,56},{32,64},{40,72},{48,80},{56,88},{64,... | collective-permute-start | bytes 129032 | tf_op jit(solution)/shard_map/ppermute | solution.py:304
  26.3 0.9 slice_bitcast_fusion
  27.2 0.1 copy.3
  27.3 0.8 broadcast_in_dim.4
  28.1 5.8 %all-to-all-start = ((bf16[8,64,328]{2,1,0:T(8,128)(2,1)}), bf16[8,64,328]{2,1,0:T(8,128)(2,1)S(1)}, u32[]{:S(2)}, u32[]{:S(2)}) async-start(bf16[8,64,328]{2,1,0:T(8,128)(2,1)} %broadcast_in_dim.4), calls=%async_computation | async-start | bytes 786432 | tf_op jit(solution)/shard_map/all_to_all | solution.py:300
  33.9 4.8 %collective-permute-start.6 = (bf16[32,2688]{1,0:T(8,128)(2,1)S(1)}, bf16[32,2688]{1,0:T(8,128)(2,1)S(1)}, u32[]{:S(2)}, u32[]{:S(2)}) collective-permute-start(bf16[32,2688]{1,0:T(8,128)(2,1)S(1)} %pad_maximum_fusion), channel_id=1, source_target_pairs={{0,256},{128,384},{256,0},{384,128},{1,257},{129,385},{257,1},{385... | collective-permute-start | bytes 516104 | tf_op jit(solution)/shard_map/ppermute | solution.py:304
  38.8 3.1 %collective-permute-start.5 = (bf16[32,2688]{1,0:T(8,128)(2,1)S(1)}, bf16[32,2688]{1,0:T(8,128)(2,1)S(1)}, u32[]{:S(2)}, u32[]{:S(2)}) collective-permute-start(bf16[32,2688]{1,0:T(8,128)(2,1)S(1)} %pad_maximum_fusion), channel_id=1, source_target_pairs={{0,16},{8,24},{16,32},{24,40},{32,48},{40,56},{48,64},{56,72},{64,... | collective-permute-start | bytes 516104 | tf_op jit(solution)/shard_map/ppermute | solution.py:304
  41.9 3.8 %collective-permute-start.4 = (bf16[32,2688]{1,0:T(8,128)(2,1)S(1)}, bf16[32,2688]{1,0:T(8,128)(2,1)S(1)}, u32[]{:S(2)}, u32[]{:S(2)}) collective-permute-start(bf16[32,2688]{1,0:T(8,128)(2,1)S(1)} %pad_maximum_fusion), channel_id=1, source_target_pairs={{0,120},{8,0},{16,8},{24,16},{32,24},{40,32},{48,40},{56,48},{64,5... | collective-permute-start | bytes 516104 | tf_op jit(solution)/shard_map/ppermute | solution.py:304
  45.7 1.9 %collective-permute-start.3 = (bf16[32,2688]{1,0:T(8,128)(2,1)S(1)}, bf16[32,2688]{1,0:T(8,128)(2,1)S(1)}, u32[]{:S(2)}, u32[]{:S(2)}) collective-permute-start(bf16[32,2688]{1,0:T(8,128)(2,1)S(1)} %pad_maximum_fusion), channel_id=1, source_target_pairs={{0,8},{8,16},{16,24},{24,32},{32,40},{40,48},{48,56},{56,64},{64,7... | collective-permute-start | bytes 516104 | tf_op jit(solution)/shard_map/ppermute | solution.py:304
  47.7 7.8 %collective-permute-done.3 = bf16[32,2688]{1,0:T(8,128)(2,1)S(1)} collective-permute-done((bf16[32,2688]{1,0:T(8,128)(2,1)S(1)}, bf16[32,2688]{1,0:T(8,128)(2,1)S(1)}, u32[]{:S(2)}, u32[]{:S(2)}) %collective-permute-start.3) | collective-permute-done | bytes 172064 | tf_op jit(solution)/shard_map/ppermute | solution.py:304
  55.7 0.1 copy.4
  55.8 0.9 broadcast_in_dim.5
  56.7 6.1 %all-to-all-start.1 = ((bf16[32,64,128]{2,1,0:T(8,128)(2,1)}), bf16[32,64,128]{2,1,0:T(8,128)(2,1)S(1)}, u32[]{:S(2)}, u32[]{:S(2)}) async-start(bf16[32,64,128]{2,1,0:T(8,128)(2,1)} %broadcast_in_dim.5), calls=%async_computation.1 | async-start | bytes 1048576 | tf_op jit(solution)/shard_map/all_to_all | solution.py:325
  62.8 1.9 %collective-permute-start.11 = (bf16[32,2688]{1,0:T(8,128)(2,1)S(1)}, bf16[32,2688]{1,0:T(8,128)(2,1)S(1)}, u32[]{:S(2)}, u32[]{:S(2)}) collective-permute-start(bf16[32,2688]{1,0:T(8,128)(2,1)S(1)} %collective-permute-done.6.x3_ref), channel_id=1, source_target_pairs={{0,16},{8,24},{16,32},{24,40},{32,48},{40,56},{48,64},{56,72},{64,... | collective-permute-start | bytes 516104 | tf_op jit(solution)/shard_map/ppermute | solution.py:304
  64.7 3.9 %collective-permute-start.10 = (bf16[32,2688]{1,0:T(8,128)(2,1)S(1)}, bf16[32,2688]{1,0:T(8,128)(2,1)S(1)}, u32[]{:S(2)}, u32[]{:S(2)}) collective-permute-start(bf16[32,2688]{1,0:T(8,128)(2,1)S(1)} %collective-permute-done.6.x3_ref), channel_id=1, source_target_pairs={{0,120},{8,0},{16,8},{24,16},{32,24},{40,32},{48,40},{56,48},{64,5... | collective-permute-start | bytes 516104 | tf_op jit(solution)/shard_map/ppermute | solution.py:304
  68.6 1.9 %collective-permute-start.9 = (bf16[32,2688]{1,0:T(8,128)(2,1)S(1)}, bf16[32,2688]{1,0:T(8,128)(2,1)}, u32[]{:S(2)}, u32[]{:S(2)}) collective-permute-start(bf16[32,2688]{1,0:T(8,128)(2,1)S(1)} %collective-permute-done.6.x3_ref), channel_id=1, source_target_pairs={{0,8},{8,16},{16,24},{24,32},{32,40},{40,48},{48,56},{56,64},{64,7... | collective-permute-start | bytes 516104 | tf_op jit(solution)/shard_map/ppermute | solution.py:304
  70.5 4.5 %collective-permute-start.8 = (bf16[128,2688]{1,0:T(8,128)(2,1)S(1)}, bf16[128,2688]{1,0:T(8,128)(2,1)S(1)}, u32[]{:S(2)}, u32[]{:S(2)}) collective-permute-start(bf16[128,2688]{1,0:T(8,128)(2,1)S(1)} %constant_dynamic-update-slice_fusion.x0_ref), channel_id=1, source_target_pairs={{0,384},{128,0},{256,128},{384,256},{1,385},{129,1},{257,129},{385... | collective-permute-start | bytes 2064392 | tf_op jit(solution)/shard_map/ppermute | solution.py:304
  75.1 1.9 %collective-permute-start.7 = (bf16[128,2688]{1,0:T(8,128)(2,1)S(1)}, bf16[128,2688]{1,0:T(8,128)(2,1)S(1)}, u32[]{:S(2)}, u32[]{:S(2)}) collective-permute-start(bf16[128,2688]{1,0:T(8,128)(2,1)S(1)} %constant_dynamic-update-slice_fusion.x0_ref), channel_id=1, source_target_pairs={{0,128},{128,256},{256,384},{384,0},{1,129},{129,257},{257,385},{3... | collective-permute-start | bytes 2064392 | tf_op jit(solution)/shard_map/ppermute | solution.py:304
  77.1 1.0 copy-done.1
  78.1 17.9 %factor.1 = (bf16[512,512]{1,0:T(8,128)(2,1)S(1)}, bf16[512,512]{1,0:T(8,128)(2,1)S(1)}, bf16[256,256]{1,0:T(8,128)(2,1)S(1)}, bf16[256,256]{1,0:T(8,128)(2,1)S(1)}, f32[8,64]{1,0:T(8,128)S(1)}) custom-call(s32[1]{0:T(128)} %bitcast.r_ref, s32[1]{0:T(128)} %bitcast.1.q_ref, bf16[4,512,128]{2,1,0:T(8,128)(2,1)S(1)} %bitcast.14, bf16[512,512]{1,0:T(8,128)(2,1)S(1)} %copy-done.1), custom_call_target="tpu_custom_call" | custom-call | flops 40000000000 | bytes 1048576 | tf_op jit(solution)/shard_map/factor/pallas_call | solution.py:253
  96.0 7.8 %update.1 = f32[328,1,1,2624]{3,2,1,0:T(1,128)} custom-call(s32[1]{0:T(128)} %bitcast.r_ref, s32[1]{0:T(128)} %bitcast.1.q_ref, bf16[512,512]{1,0:T(8,128)(2,1)S(1)} %get-tuple-element.17.head_ref, bf16[512,512]{1,0:T(8,128)(2,1)S(1)} %get-tuple-element.18.side_ref, bf16[256,256]{1,0:T(8,128)(2,1)S(1)} %get-tuple-element.19.g_ref, ...), custom_call_target="tpu_custom_call" | custom-call | tf_op jit(solution)/shard_map/update/pallas_call | solution.py:276
  (25 shorter events, 0.2 us)
Async XLA Ops:
  0.8 33.1 %collective-permute-start.2 = (bf16[8,2688]{1,0:T(8,128)(2,1)S(1)}, bf16[8,2688]{1,0:T(8,128)(2,1)S(1)}, u32[]{:S(2)}, u32[]{:S(2)}) collective-permute-start(bf16[8,2688]{1,0:T(8,128)(2,1)S(1)} %get-tuple-element.25), channel_id=1, source_target_pairs={{0,64},{8,72},{16,80},{24,88},{32,96},{40,104},{48,112},{56,120},{... | collective-permute-start | bytes 129032 | tf_op jit(solution)/shard_map/ppermute | solution.py:304
  17.1 16.8 %collective-permute-start.1 = (bf16[8,2688]{1,0:T(8,128)(2,1)S(1)}, bf16[8,2688]{1,0:T(8,128)(2,1)S(1)}, u32[]{:S(2)}, u32[]{:S(2)}) collective-permute-start(bf16[8,2688]{1,0:T(8,128)(2,1)S(1)} %get-tuple-element.25), channel_id=1, source_target_pairs={{0,96},{8,104},{16,112},{24,120},{32,0},{40,8},{48,16},{56,24},{64... | collective-permute-start | bytes 129032 | tf_op jit(solution)/shard_map/ppermute | solution.py:304
  19.0 14.9 %collective-permute-start = (bf16[8,2688]{1,0:T(8,128)(2,1)S(1)}, bf16[8,2688]{1,0:T(8,128)(2,1)S(1)}, u32[]{:S(2)}, u32[]{:S(2)}) collective-permute-start(bf16[8,2688]{1,0:T(8,128)(2,1)S(1)} %get-tuple-element.25), channel_id=1, source_target_pairs={{0,32},{8,40},{16,48},{24,56},{32,64},{40,72},{48,80},{56,88},{64,... | collective-permute-start | bytes 129032 | tf_op jit(solution)/shard_map/ppermute | solution.py:304
  28.1 27.6 %all-to-all-start = ((bf16[8,64,328]{2,1,0:T(8,128)(2,1)}), bf16[8,64,328]{2,1,0:T(8,128)(2,1)S(1)}, u32[]{:S(2)}, u32[]{:S(2)}) async-start(bf16[8,64,328]{2,1,0:T(8,128)(2,1)} %broadcast_in_dim.4), calls=%async_computation | async-start | bytes 786432 | tf_op jit(solution)/shard_map/all_to_all | solution.py:300
  33.9 21.8 %collective-permute-start.6 = (bf16[32,2688]{1,0:T(8,128)(2,1)S(1)}, bf16[32,2688]{1,0:T(8,128)(2,1)S(1)}, u32[]{:S(2)}, u32[]{:S(2)}) collective-permute-start(bf16[32,2688]{1,0:T(8,128)(2,1)S(1)} %pad_maximum_fusion), channel_id=1, source_target_pairs={{0,256},{128,384},{256,0},{384,128},{1,257},{129,385},{257,1},{385... | collective-permute-start | bytes 516104 | tf_op jit(solution)/shard_map/ppermute | solution.py:304
  38.8 16.8 %collective-permute-start.5 = (bf16[32,2688]{1,0:T(8,128)(2,1)S(1)}, bf16[32,2688]{1,0:T(8,128)(2,1)S(1)}, u32[]{:S(2)}, u32[]{:S(2)}) collective-permute-start(bf16[32,2688]{1,0:T(8,128)(2,1)S(1)} %pad_maximum_fusion), channel_id=1, source_target_pairs={{0,16},{8,24},{16,32},{24,40},{32,48},{40,56},{48,64},{56,72},{64,... | collective-permute-start | bytes 516104 | tf_op jit(solution)/shard_map/ppermute | solution.py:304
  41.9 13.7 %collective-permute-start.4 = (bf16[32,2688]{1,0:T(8,128)(2,1)S(1)}, bf16[32,2688]{1,0:T(8,128)(2,1)S(1)}, u32[]{:S(2)}, u32[]{:S(2)}) collective-permute-start(bf16[32,2688]{1,0:T(8,128)(2,1)S(1)} %pad_maximum_fusion), channel_id=1, source_target_pairs={{0,120},{8,0},{16,8},{24,16},{32,24},{40,32},{48,40},{56,48},{64,5... | collective-permute-start | bytes 516104 | tf_op jit(solution)/shard_map/ppermute | solution.py:304
  45.7 9.8 %collective-permute-start.3 = (bf16[32,2688]{1,0:T(8,128)(2,1)S(1)}, bf16[32,2688]{1,0:T(8,128)(2,1)S(1)}, u32[]{:S(2)}, u32[]{:S(2)}) collective-permute-start(bf16[32,2688]{1,0:T(8,128)(2,1)S(1)} %pad_maximum_fusion), channel_id=1, source_target_pairs={{0,8},{8,16},{16,24},{24,32},{32,40},{40,48},{48,56},{56,64},{64,7... | collective-permute-start | bytes 516104 | tf_op jit(solution)/shard_map/ppermute | solution.py:304
  56.7 20.4 %all-to-all-start.1 = ((bf16[32,64,128]{2,1,0:T(8,128)(2,1)}), bf16[32,64,128]{2,1,0:T(8,128)(2,1)S(1)}, u32[]{:S(2)}, u32[]{:S(2)}) async-start(bf16[32,64,128]{2,1,0:T(8,128)(2,1)} %broadcast_in_dim.5), calls=%async_computation.1 | async-start | bytes 1048576 | tf_op jit(solution)/shard_map/all_to_all | solution.py:325
  62.8 33.2 %collective-permute-start.11 = (bf16[32,2688]{1,0:T(8,128)(2,1)S(1)}, bf16[32,2688]{1,0:T(8,128)(2,1)S(1)}, u32[]{:S(2)}, u32[]{:S(2)}) collective-permute-start(bf16[32,2688]{1,0:T(8,128)(2,1)S(1)} %collective-permute-done.6.x3_ref), channel_id=1, source_target_pairs={{0,16},{8,24},{16,32},{24,40},{32,48},{40,56},{48,64},{56,72},{64,... | collective-permute-start | bytes 516104 | tf_op jit(solution)/shard_map/ppermute | solution.py:304
  64.7 31.3 %collective-permute-start.10 = (bf16[32,2688]{1,0:T(8,128)(2,1)S(1)}, bf16[32,2688]{1,0:T(8,128)(2,1)S(1)}, u32[]{:S(2)}, u32[]{:S(2)}) collective-permute-start(bf16[32,2688]{1,0:T(8,128)(2,1)S(1)} %collective-permute-done.6.x3_ref), channel_id=1, source_target_pairs={{0,120},{8,0},{16,8},{24,16},{32,24},{40,32},{48,40},{56,48},{64,5... | collective-permute-start | bytes 516104 | tf_op jit(solution)/shard_map/ppermute | solution.py:304
  68.6 27.4 %collective-permute-start.9 = (bf16[32,2688]{1,0:T(8,128)(2,1)S(1)}, bf16[32,2688]{1,0:T(8,128)(2,1)}, u32[]{:S(2)}, u32[]{:S(2)}) collective-permute-start(bf16[32,2688]{1,0:T(8,128)(2,1)S(1)} %collective-permute-done.6.x3_ref), channel_id=1, source_target_pairs={{0,8},{8,16},{16,24},{24,32},{32,40},{40,48},{48,56},{56,64},{64,7... | collective-permute-start | bytes 516104 | tf_op jit(solution)/shard_map/ppermute | solution.py:304
  70.5 25.5 %collective-permute-start.8 = (bf16[128,2688]{1,0:T(8,128)(2,1)S(1)}, bf16[128,2688]{1,0:T(8,128)(2,1)S(1)}, u32[]{:S(2)}, u32[]{:S(2)}) collective-permute-start(bf16[128,2688]{1,0:T(8,128)(2,1)S(1)} %constant_dynamic-update-slice_fusion.x0_ref), channel_id=1, source_target_pairs={{0,384},{128,0},{256,128},{384,256},{1,385},{129,1},{257,129},{385... | collective-permute-start | bytes 2064392 | tf_op jit(solution)/shard_map/ppermute | solution.py:304
  75.1 20.9 %collective-permute-start.7 = (bf16[128,2688]{1,0:T(8,128)(2,1)S(1)}, bf16[128,2688]{1,0:T(8,128)(2,1)S(1)}, u32[]{:S(2)}, u32[]{:S(2)}) collective-permute-start(bf16[128,2688]{1,0:T(8,128)(2,1)S(1)} %constant_dynamic-update-slice_fusion.x0_ref), channel_id=1, source_target_pairs={{0,128},{128,256},{256,384},{384,0},{1,129},{129,257},{257,385},{3... | collective-permute-start | bytes 2064392 | tf_op jit(solution)/shard_map/ppermute | solution.py:304
  77.0 1.0 %copy-start.1 = (bf16[512,512]{1,0:T(8,128)(2,1)S(1)}, bf16[512,512]{1,0:T(8,128)(2,1)}, u32[]{:S(2)}) copy-start(bf16[512,512]{1,0:T(8,128)(2,1)} %constant.30.clone.pcol_ref) | copy-start | bytes 1572868
  78.1 17.9 %copy-start = (bf16[328,1,1,2624]{3,0,2,1:T(8,128)(2,1)S(1)}, bf16[328,1,1,2624]{3,0,2,1:T(8,128)(2,1)}, u32[]{:S(2)}) copy-start(bf16[328,1,1,2624]{3,0,2,1:T(8,128)(2,1)} %param.2) | copy-start | bytes 5164036

commit v5 on v4

--- a/solution.py
+++ b/solution.py
@@ -1,8 +1,5 @@
-import functools
-
 import jax
 import jax.numpy as jnp
-import numpy as np
 from jax import lax
 from jax.experimental import pallas as pl
 from jax.experimental.pallas import tpu as pltpu
@@ -128,18 +125,21 @@
     return jnp.broadcast_to(order[0:1, :], (B, T))
 
 
-def factor_kernel(r_ref, q_ref, x_ref, pcol_ref, head_ref, side_ref, g_ref, l_ref, own_ref, u_scr, a_scr):
+def factor_kernel(r_ref, q_ref, x_ref, head_ref, side_ref, g_ref, l_ref, own_ref, u_scr, a_scr):
     r = r_ref[0]
     q = q_ref[0]
     rows = lax.broadcasted_iota(jnp.int32, (B, T), 0)
     order = natural_rows(r, True)
     prow = jnp.concatenate([(rows == order).astype(BF16), (rows + B == order).astype(BF16)], axis=0)
     flat = jnp.concatenate([x_ref[y] for y in range(NY)], axis=1)
-    part = mm(pcol_ref[...], flat).astype(BF16)
+    stored = lax.broadcasted_iota(jnp.int32, (8, T), 1)
+    column = jnp.broadcast_to((lax.rem(stored, LC) * COLS + stored // LC)[0:1, :], (B, T))
+    pcol = [(rows == column).astype(BF16), (rows + B == column).astype(BF16)]
+    part = mm(jnp.concatenate(pcol, axis=0), flat).astype(BF16)
     a_scr[...] = mm(part, prow, 1, 1)
     order = natural_rows(r, False)
     head_ref[B:T, :] = (rows + B == order).astype(BF16)
-    side_ref[B:T, :] = pcol_ref[B:T, :]
+    side_ref[B:T, :] = pcol[1]
     u1, g1 = factor_panel(a_scr[0:B, 0:B])
     g1b = g1.astype(BF16)
     s21 = mm(a_scr[B:T, 0:B].astype(BF16), g1b, 1, 1)
@@ -148,7 +148,7 @@
     s12 = mm(g1b, a_scr[0:B, B:T].astype(BF16), 1, 0)
     l_ref[...] = s21b
     head_ref[0:B, :] = mm(g1b, (rows == order).astype(BF16)).astype(BF16)
-    side_ref[0:B, :] = mm(g1b, pcol_ref[0:B, :]).astype(BF16)
+    side_ref[0:B, :] = mm(g1b, pcol[0]).astype(BF16)
     for k in range(B // LANE):
         lanes = slice(LANE * k, LANE * k + LANE)
         u_scr[k, 0:B, :] = u1.T[:, lanes]
@@ -241,14 +241,7 @@
         copy.wait()
 
 
-def column_order():
-    nat = np.arange(T)
-    pcol = np.zeros((T, T), np.float32)
-    pcol[nat, (nat % COLS) * LC + nat // COLS] = 1
-    return pcol.astype(jnp.bfloat16)
-
-
-def factor(pos, corner, pcol):
+def factor(pos, corner):
     vmem = pl.BlockSpec(memory_space=pltpu.VMEM)
     return pl.pallas_call(
         factor_kernel,
@@ -259,13 +252,13 @@
             jax.ShapeDtypeStruct((B, B), BF16),
             jax.ShapeDtypeStruct((LR, LC), F32),
         ),
-        in_specs=[pl.BlockSpec(memory_space=pltpu.SMEM)] * 2 + [vmem] * 2,
+        in_specs=[pl.BlockSpec(memory_space=pltpu.SMEM)] * 2 + [vmem],
         out_specs=(vmem,) * 5,
         scratch_shapes=[pltpu.VMEM((T // LANE, T, LANE), F32), pltpu.VMEM((T, T), F32)],
         cost_estimate=pl.CostEstimate(flops=40_000_000_000, transcendentals=0, bytes_accessed=4 * T * T),
         compiler_params=pltpu.CompilerParams(vmem_limit_bytes=24 << 20),
         name="factor",
-    )(*pos, corner, pcol)
+    )(*pos, corner)
 
 
 def update(pos, head, side, g2, l21, own, wr, xs, w):
@@ -311,7 +304,6 @@
     r = lax.axis_index(("y", "zh", "zl"))
     q = lax.axis_index(("x", "c"))
     pos = (r.reshape(1).astype(jnp.int32), q.reshape(1).astype(jnp.int32))
-    pcol = jnp.asarray(column_order())
     head_rows = jnp.pad(work[0:LR, :], ((0, 0), (0, -cols % LANE)))
 
     wr = everyone(jnp.transpose(work[:, 0:LC]), ("x", "c"), COLS).reshape(T, rows)
@@ -325,7 +317,7 @@
     corner = lax.all_to_all(pieces, ("y", "x", "c"), 0, 0, tiled=True).reshape(NY, T, NZ * LR)
     xs = spread(x, "y", NY, NEAR[:2]) + spread(across, ("zh", "zl"), NZ, NEAR)
 
-    head, side, g2, l21, own = factor(pos, corner, pcol)
+    head, side, g2, l21, own = factor(pos, corner)
     return update(pos, head, side, g2, l21, own, wr, xs, work)
 
 

time: 105 us -> 104 us (level)
  no operation moved by 1% of the time
where the time goes in v5:
time: 104 us; the launch traced here: 103 us
  starting transfers between devices  65.3 us (63%)
  Pallas kernels  25.7 us (25%)
  waiting for transfers between devices  7.88 us (8%)
  local copies, waits for them, and re-layouts  3.69 us (4%)
    ppermute x12, starting transfers between devices, spread(): lax.ppermute(x, axis, [(i, (i + d) % count) for i in range(count)])  53.4 us
    pallas_call x1, Pallas kernels, factor(): pl.pallas_call(factor_kernel, out_shape=(jax.ShapeDtypeStruct((T, T), BF1...  17.9 us
    ppermute x12, waiting for transfers between devices, spread(): lax.ppermute(x, axis, [(i, (i + d) % count) for i in range(count)])  7.88 us
    pallas_call x1, Pallas kernels, update(): pl.pallas_call(update_kernel, grid=(1,), out_shape=jax.ShapeDtypeStruct((...  7.8 us
    all_to_all x1, starting transfers between devices, on_device(): lax.all_to_all(pieces, ('y', 'x', 'c'), 0, 0, tiled=True)  6.06 us
    all_to_all x1, starting transfers between devices, everyone(): lax.all_to_all(jnp.broadcast_to(x[None], (count,) + x.shape), axis, 0, 0,...  5.81 us
  transfers between devices with their start and end apart: 14, of which 1 were waited for; matrix products, arithmetic and copies ran while one was open for 2% of the time, Pallas kernels for 17%

profile of v5, /device:TPU:1, one launch (start us, length us, event | category | flops | bytes accessed | tf_op | source)
XLA Modules:
  0.0 103.0 jit_solution(7119419035394616209)
XLA Ops:
  0.0 0.8 slice_bitcast_fusion.1
  0.8 16.3 %collective-permute-start.2 = (bf16[8,2688]{1,0:T(8,128)(2,1)S(1)}, bf16[8,2688]{1,0:T(8,128)(2,1)S(1)}, u32[]{:S(2)}, u32[]{:S(2)}) collective-permute-start(bf16[8,2688]{1,0:T(8,128)(2,1)S(1)} %get-tuple-element.25), channel_id=1, source_target_pairs={{0,64},{8,72},{16,80},{24,88},{32,96},{40,104},{48,112},{56,120},{... | collective-permute-start | bytes 129032 | tf_op jit(solution)/shard_map/ppermute | solution.py:297
  17.1 1.9 %collective-permute-start.1 = (bf16[8,2688]{1,0:T(8,128)(2,1)S(1)}, bf16[8,2688]{1,0:T(8,128)(2,1)S(1)}, u32[]{:S(2)}, u32[]{:S(2)}) collective-permute-start(bf16[8,2688]{1,0:T(8,128)(2,1)S(1)} %get-tuple-element.25), channel_id=1, source_target_pairs={{0,96},{8,104},{16,112},{24,120},{32,0},{40,8},{48,16},{56,24},{64... | collective-permute-start | bytes 129032 | tf_op jit(solution)/shard_map/ppermute | solution.py:297
  19.0 7.3 %collective-permute-start = (bf16[8,2688]{1,0:T(8,128)(2,1)S(1)}, bf16[8,2688]{1,0:T(8,128)(2,1)S(1)}, u32[]{:S(2)}, u32[]{:S(2)}) collective-permute-start(bf16[8,2688]{1,0:T(8,128)(2,1)S(1)} %get-tuple-element.25), channel_id=1, source_target_pairs={{0,32},{8,40},{16,48},{24,56},{32,64},{40,72},{48,80},{56,88},{64,... | collective-permute-start | bytes 129032 | tf_op jit(solution)/shard_map/ppermute | solution.py:297
  26.3 0.9 slice_bitcast_fusion
  27.2 0.1 copy.2
  27.3 0.8 broadcast_in_dim.4
  28.1 5.8 %all-to-all-start = ((bf16[8,64,328]{2,1,0:T(8,128)(2,1)}), bf16[8,64,328]{2,1,0:T(8,128)(2,1)S(1)}, u32[]{:S(2)}, u32[]{:S(2)}) async-start(bf16[8,64,328]{2,1,0:T(8,128)(2,1)} %broadcast_in_dim.4), calls=%async_computation | async-start | bytes 786432 | tf_op jit(solution)/shard_map/all_to_all | solution.py:293
  33.9 4.8 %collective-permute-start.6 = (bf16[32,2688]{1,0:T(8,128)(2,1)S(1)}, bf16[32,2688]{1,0:T(8,128)(2,1)S(1)}, u32[]{:S(2)}, u32[]{:S(2)}) collective-permute-start(bf16[32,2688]{1,0:T(8,128)(2,1)S(1)} %pad_maximum_fusion), channel_id=1, source_target_pairs={{0,256},{128,384},{256,0},{384,128},{1,257},{129,385},{257,1},{385... | collective-permute-start | bytes 516104 | tf_op jit(solution)/shard_map/ppermute | solution.py:297
  38.8 3.1 %collective-permute-start.5 = (bf16[32,2688]{1,0:T(8,128)(2,1)S(1)}, bf16[32,2688]{1,0:T(8,128)(2,1)S(1)}, u32[]{:S(2)}, u32[]{:S(2)}) collective-permute-start(bf16[32,2688]{1,0:T(8,128)(2,1)S(1)} %pad_maximum_fusion), channel_id=1, source_target_pairs={{0,16},{8,24},{16,32},{24,40},{32,48},{40,56},{48,64},{56,72},{64,... | collective-permute-start | bytes 516104 | tf_op jit(solution)/shard_map/ppermute | solution.py:297
  41.9 3.8 %collective-permute-start.4 = (bf16[32,2688]{1,0:T(8,128)(2,1)S(1)}, bf16[32,2688]{1,0:T(8,128)(2,1)S(1)}, u32[]{:S(2)}, u32[]{:S(2)}) collective-permute-start(bf16[32,2688]{1,0:T(8,128)(2,1)S(1)} %pad_maximum_fusion), channel_id=1, source_target_pairs={{0,120},{8,0},{16,8},{24,16},{32,24},{40,32},{48,40},{56,48},{64,5... | collective-permute-start | bytes 516104 | tf_op jit(solution)/shard_map/ppermute | solution.py:297
  45.7 1.9 %collective-permute-start.3 = (bf16[32,2688]{1,0:T(8,128)(2,1)S(1)}, bf16[32,2688]{1,0:T(8,128)(2,1)S(1)}, u32[]{:S(2)}, u32[]{:S(2)}) collective-permute-start(bf16[32,2688]{1,0:T(8,128)(2,1)S(1)} %pad_maximum_fusion), channel_id=1, source_target_pairs={{0,8},{8,16},{16,24},{24,32},{32,40},{40,48},{48,56},{56,64},{64,7... | collective-permute-start | bytes 516104 | tf_op jit(solution)/shard_map/ppermute | solution.py:297
  47.7 7.8 %collective-permute-done.3 = bf16[32,2688]{1,0:T(8,128)(2,1)S(1)} collective-permute-done((bf16[32,2688]{1,0:T(8,128)(2,1)S(1)}, bf16[32,2688]{1,0:T(8,128)(2,1)S(1)}, u32[]{:S(2)}, u32[]{:S(2)}) %collective-permute-start.3) | collective-permute-done | bytes 172064 | tf_op jit(solution)/shard_map/ppermute | solution.py:297
  55.7 0.1 copy.3
  55.8 0.9 broadcast_in_dim.5
  56.7 6.1 %all-to-all-start.1 = ((bf16[32,64,128]{2,1,0:T(8,128)(2,1)}), bf16[32,64,128]{2,1,0:T(8,128)(2,1)S(1)}, u32[]{:S(2)}, u32[]{:S(2)}) async-start(bf16[32,64,128]{2,1,0:T(8,128)(2,1)} %broadcast_in_dim.5), calls=%async_computation.1 | async-start | bytes 1048576 | tf_op jit(solution)/shard_map/all_to_all | solution.py:317
  62.8 1.9 %collective-permute-start.11 = (bf16[32,2688]{1,0:T(8,128)(2,1)S(1)}, bf16[32,2688]{1,0:T(8,128)(2,1)S(1)}, u32[]{:S(2)}, u32[]{:S(2)}) collective-permute-start(bf16[32,2688]{1,0:T(8,128)(2,1)S(1)} %collective-permute-done.6.x3_ref), channel_id=1, source_target_pairs={{0,16},{8,24},{16,32},{24,40},{32,48},{40,56},{48,64},{56,72},{64,... | collective-permute-start | bytes 516104 | tf_op jit(solution)/shard_map/ppermute | solution.py:297
  64.7 3.9 %collective-permute-start.10 = (bf16[32,2688]{1,0:T(8,128)(2,1)S(1)}, bf16[32,2688]{1,0:T(8,128)(2,1)S(1)}, u32[]{:S(2)}, u32[]{:S(2)}) collective-permute-start(bf16[32,2688]{1,0:T(8,128)(2,1)S(1)} %collective-permute-done.6.x3_ref), channel_id=1, source_target_pairs={{0,120},{8,0},{16,8},{24,16},{32,24},{40,32},{48,40},{56,48},{64,5... | collective-permute-start | bytes 516104 | tf_op jit(solution)/shard_map/ppermute | solution.py:297
  68.6 1.9 %collective-permute-start.9 = (bf16[32,2688]{1,0:T(8,128)(2,1)S(1)}, bf16[32,2688]{1,0:T(8,128)(2,1)}, u32[]{:S(2)}, u32[]{:S(2)}) collective-permute-start(bf16[32,2688]{1,0:T(8,128)(2,1)S(1)} %collective-permute-done.6.x3_ref), channel_id=1, source_target_pairs={{0,8},{8,16},{16,24},{24,32},{32,40},{40,48},{48,56},{56,64},{64,7... | collective-permute-start | bytes 516104 | tf_op jit(solution)/shard_map/ppermute | solution.py:297
  70.5 4.5 %collective-permute-start.8 = (bf16[128,2688]{1,0:T(8,128)(2,1)S(1)}, bf16[128,2688]{1,0:T(8,128)(2,1)S(1)}, u32[]{:S(2)}, u32[]{:S(2)}) collective-permute-start(bf16[128,2688]{1,0:T(8,128)(2,1)S(1)} %constant_dynamic-update-slice_fusion.x0_ref), channel_id=1, source_target_pairs={{0,384},{128,0},{256,128},{384,256},{1,385},{129,1},{257,129},{385... | collective-permute-start | bytes 2064392 | tf_op jit(solution)/shard_map/ppermute | solution.py:297
  75.1 1.9 %collective-permute-start.7 = (bf16[128,2688]{1,0:T(8,128)(2,1)S(1)}, bf16[128,2688]{1,0:T(8,128)(2,1)S(1)}, u32[]{:S(2)}, u32[]{:S(2)}) collective-permute-start(bf16[128,2688]{1,0:T(8,128)(2,1)S(1)} %constant_dynamic-update-slice_fusion.x0_ref), channel_id=1, source_target_pairs={{0,128},{128,256},{256,384},{384,0},{1,129},{129,257},{257,385},{3... | collective-permute-start | bytes 2064392 | tf_op jit(solution)/shard_map/ppermute | solution.py:297
  77.1 17.9 %factor.1 = (bf16[512,512]{1,0:T(8,128)(2,1)S(1)}, bf16[512,512]{1,0:T(8,128)(2,1)S(1)}, bf16[256,256]{1,0:T(8,128)(2,1)S(1)}, bf16[256,256]{1,0:T(8,128)(2,1)S(1)}, f32[8,64]{1,0:T(8,128)S(1)}) custom-call(s32[1]{0:T(128)} %bitcast.r_ref, s32[1]{0:T(128)} %bitcast.1.q_ref, bf16[4,512,128]{2,1,0:T(8,128)(2,1)S(1)} %bitcast.14), custom_call_target="tpu_custom_call" | custom-call | flops 40000000000 | bytes 1048576 | tf_op jit(solution)/shard_map/factor/pallas_call | solution.py:246
  95.0 0.0 collective-permute-done.10.x5_ref
  95.0 7.8 %update.1 = f32[328,1,1,2624]{3,2,1,0:T(1,128)} custom-call(s32[1]{0:T(128)} %bitcast.r_ref, s32[1]{0:T(128)} %bitcast.1.q_ref, bf16[512,512]{1,0:T(8,128)(2,1)S(1)} %get-tuple-element.17.head_ref, bf16[512,512]{1,0:T(8,128)(2,1)S(1)} %get-tuple-element.18.side_ref, bf16[256,256]{1,0:T(8,128)(2,1)S(1)} %get-tuple-element.19.g_ref, ...), custom_call_target="tpu_custom_call" | custom-call | tf_op jit(solution)/shard_map/update/pallas_call | solution.py:269
  (23 shorter events, 0.2 us)
Async XLA Ops:
  0.8 33.1 %collective-permute-start.2 = (bf16[8,2688]{1,0:T(8,128)(2,1)S(1)}, bf16[8,2688]{1,0:T(8,128)(2,1)S(1)}, u32[]{:S(2)}, u32[]{:S(2)}) collective-permute-start(bf16[8,2688]{1,0:T(8,128)(2,1)S(1)} %get-tuple-element.25), channel_id=1, source_target_pairs={{0,64},{8,72},{16,80},{24,88},{32,96},{40,104},{48,112},{56,120},{... | collective-permute-start | bytes 129032 | tf_op jit(solution)/shard_map/ppermute | solution.py:297
  17.1 16.8 %collective-permute-start.1 = (bf16[8,2688]{1,0:T(8,128)(2,1)S(1)}, bf16[8,2688]{1,0:T(8,128)(2,1)S(1)}, u32[]{:S(2)}, u32[]{:S(2)}) collective-permute-start(bf16[8,2688]{1,0:T(8,128)(2,1)S(1)} %get-tuple-element.25), channel_id=1, source_target_pairs={{0,96},{8,104},{16,112},{24,120},{32,0},{40,8},{48,16},{56,24},{64... | collective-permute-start | bytes 129032 | tf_op jit(solution)/shard_map/ppermute | solution.py:297
  19.0 14.9 %collective-permute-start = (bf16[8,2688]{1,0:T(8,128)(2,1)S(1)}, bf16[8,2688]{1,0:T(8,128)(2,1)S(1)}, u32[]{:S(2)}, u32[]{:S(2)}) collective-permute-start(bf16[8,2688]{1,0:T(8,128)(2,1)S(1)} %get-tuple-element.25), channel_id=1, source_target_pairs={{0,32},{8,40},{16,48},{24,56},{32,64},{40,72},{48,80},{56,88},{64,... | collective-permute-start | bytes 129032 | tf_op jit(solution)/shard_map/ppermute | solution.py:297
  28.1 27.6 %all-to-all-start = ((bf16[8,64,328]{2,1,0:T(8,128)(2,1)}), bf16[8,64,328]{2,1,0:T(8,128)(2,1)S(1)}, u32[]{:S(2)}, u32[]{:S(2)}) async-start(bf16[8,64,328]{2,1,0:T(8,128)(2,1)} %broadcast_in_dim.4), calls=%async_computation | async-start | bytes 786432 | tf_op jit(solution)/shard_map/all_to_all | solution.py:293
  33.9 21.8 %collective-permute-start.6 = (bf16[32,2688]{1,0:T(8,128)(2,1)S(1)}, bf16[32,2688]{1,0:T(8,128)(2,1)S(1)}, u32[]{:S(2)}, u32[]{:S(2)}) collective-permute-start(bf16[32,2688]{1,0:T(8,128)(2,1)S(1)} %pad_maximum_fusion), channel_id=1, source_target_pairs={{0,256},{128,384},{256,0},{384,128},{1,257},{129,385},{257,1},{385... | collective-permute-start | bytes 516104 | tf_op jit(solution)/shard_map/ppermute | solution.py:297
  38.8 16.8 %collective-permute-start.5 = (bf16[32,2688]{1,0:T(8,128)(2,1)S(1)}, bf16[32,2688]{1,0:T(8,128)(2,1)S(1)}, u32[]{:S(2)}, u32[]{:S(2)}) collective-permute-start(bf16[32,2688]{1,0:T(8,128)(2,1)S(1)} %pad_maximum_fusion), channel_id=1, source_target_pairs={{0,16},{8,24},{16,32},{24,40},{32,48},{40,56},{48,64},{56,72},{64,... | collective-permute-start | bytes 516104 | tf_op jit(solution)/shard_map/ppermute | solution.py:297
  41.9 13.7 %collective-permute-start.4 = (bf16[32,2688]{1,0:T(8,128)(2,1)S(1)}, bf16[32,2688]{1,0:T(8,128)(2,1)S(1)}, u32[]{:S(2)}, u32[]{:S(2)}) collective-permute-start(bf16[32,2688]{1,0:T(8,128)(2,1)S(1)} %pad_maximum_fusion), channel_id=1, source_target_pairs={{0,120},{8,0},{16,8},{24,16},{32,24},{40,32},{48,40},{56,48},{64,5... | collective-permute-start | bytes 516104 | tf_op jit(solution)/shard_map/ppermute | solution.py:297
  45.7 9.8 %collective-permute-start.3 = (bf16[32,2688]{1,0:T(8,128)(2,1)S(1)}, bf16[32,2688]{1,0:T(8,128)(2,1)S(1)}, u32[]{:S(2)}, u32[]{:S(2)}) collective-permute-start(bf16[32,2688]{1,0:T(8,128)(2,1)S(1)} %pad_maximum_fusion), channel_id=1, source_target_pairs={{0,8},{8,16},{16,24},{24,32},{32,40},{40,48},{48,56},{56,64},{64,7... | collective-permute-start | bytes 516104 | tf_op jit(solution)/shard_map/ppermute | solution.py:297
  56.7 20.4 %all-to-all-start.1 = ((bf16[32,64,128]{2,1,0:T(8,128)(2,1)}), bf16[32,64,128]{2,1,0:T(8,128)(2,1)S(1)}, u32[]{:S(2)}, u32[]{:S(2)}) async-start(bf16[32,64,128]{2,1,0:T(8,128)(2,1)} %broadcast_in_dim.5), calls=%async_computation.1 | async-start | bytes 1048576 | tf_op jit(solution)/shard_map/all_to_all | solution.py:317
  62.8 32.2 %collective-permute-start.11 = (bf16[32,2688]{1,0:T(8,128)(2,1)S(1)}, bf16[32,2688]{1,0:T(8,128)(2,1)S(1)}, u32[]{:S(2)}, u32[]{:S(2)}) collective-permute-start(bf16[32,2688]{1,0:T(8,128)(2,1)S(1)} %collective-permute-done.6.x3_ref), channel_id=1, source_target_pairs={{0,16},{8,24},{16,32},{24,40},{32,48},{40,56},{48,64},{56,72},{64,... | collective-permute-start | bytes 516104 | tf_op jit(solution)/shard_map/ppermute | solution.py:297
  64.7 30.3 %collective-permute-start.10 = (bf16[32,2688]{1,0:T(8,128)(2,1)S(1)}, bf16[32,2688]{1,0:T(8,128)(2,1)S(1)}, u32[]{:S(2)}, u32[]{:S(2)}) collective-permute-start(bf16[32,2688]{1,0:T(8,128)(2,1)S(1)} %collective-permute-done.6.x3_ref), channel_id=1, source_target_pairs={{0,120},{8,0},{16,8},{24,16},{32,24},{40,32},{48,40},{56,48},{64,5... | collective-permute-start | bytes 516104 | tf_op jit(solution)/shard_map/ppermute | solution.py:297
  68.6 26.4 %collective-permute-start.9 = (bf16[32,2688]{1,0:T(8,128)(2,1)S(1)}, bf16[32,2688]{1,0:T(8,128)(2,1)}, u32[]{:S(2)}, u32[]{:S(2)}) collective-permute-start(bf16[32,2688]{1,0:T(8,128)(2,1)S(1)} %collective-permute-done.6.x3_ref), channel_id=1, source_target_pairs={{0,8},{8,16},{16,24},{24,32},{32,40},{40,48},{48,56},{56,64},{64,7... | collective-permute-start | bytes 516104 | tf_op jit(solution)/shard_map/ppermute | solution.py:297
  70.5 24.4 %collective-permute-start.8 = (bf16[128,2688]{1,0:T(8,128)(2,1)S(1)}, bf16[128,2688]{1,0:T(8,128)(2,1)S(1)}, u32[]{:S(2)}, u32[]{:S(2)}) collective-permute-start(bf16[128,2688]{1,0:T(8,128)(2,1)S(1)} %constant_dynamic-update-slice_fusion.x0_ref), channel_id=1, source_target_pairs={{0,384},{128,0},{256,128},{384,256},{1,385},{129,1},{257,129},{385... | collective-permute-start | bytes 2064392 | tf_op jit(solution)/shard_map/ppermute | solution.py:297
  75.1 19.9 %collective-permute-start.7 = (bf16[128,2688]{1,0:T(8,128)(2,1)S(1)}, bf16[128,2688]{1,0:T(8,128)(2,1)S(1)}, u32[]{:S(2)}, u32[]{:S(2)}) collective-permute-start(bf16[128,2688]{1,0:T(8,128)(2,1)S(1)} %constant_dynamic-update-slice_fusion.x0_ref), channel_id=1, source_target_pairs={{0,128},{128,256},{256,384},{384,0},{1,129},{129,257},{257,385},{3... | collective-permute-start | bytes 2064392 | tf_op jit(solution)/shard_map/ppermute | solution.py:297
  77.0 18.0 %copy-start = (bf16[328,1,1,2624]{3,0,2,1:T(8,128)(2,1)S(1)}, bf16[328,1,1,2624]{3,0,2,1:T(8,128)(2,1)}, u32[]{:S(2)}) copy-start(bf16[328,1,1,2624]{3,0,2,1:T(8,128)(2,1)} %param.1) | copy-start | bytes 5164036
